TPU v7x, 512 devices: a whole 4x8x8 slice. The times are simulated.
512 devices in a mesh: gy: 16 (over z, core), gx: 32 (over y, x).
Axes of the slice: x: 4, y: 8, z: 8, core: 2. Of those that a mesh axis runs over, the one named last changes fastest.
Arguments:
- atm_flux: bfloat16 [16, 64, 2, 128], P('gy', 'gx'), may hold values from -6 to 6
- remap_source: int32 [256, 32, 2], P('gy', 'gx'), may hold values from 0 to 5
- remap_weight: bfloat16 [256, 32, 2, 128, 128], P('gy', 'gx'), may hold values from -0.375 to 0.375
- tracers: float32 [2, 62, 256, 4096], P(None, None, 'gy', 'gx'), may hold values from -6 to 6
- velocity: float32 [2, 62, 256, 4096], P(None, None, 'gy', 'gx'), may hold values from -1.5 to 1.5
- vert_diff: float32 [61, 256, 4096], P(None, 'gy', 'gx'), may hold values from 0.05 to 5
- ocean_depth: float32 [256, 4096], P('gy', 'gx'), may hold values from 0.25 to 1
- surface_term: float32 [256, 4096], P('gy', 'gx'), may hold values from 0.05 to 0.5
- land_mask: int32 [64, 32], P('gy', 'gx'), may hold values from 0 to 1, as said below
- barotropic_block_map: int32 [16, 96], P('gy'), may hold values from -1 to 127, as said below
Outputs:
- new_tracers: float32 [2, 62, 256, 4096], P(None, None, 'gy', 'gx')
- sea_level: float32 [16, 96, 4, 128], P('gy', 'gx')
- barotropic_slot_residual: float32 [16, 96, 4, 128], P('gy', 'gx')
Inputs may be any that keep to these rules, and one draw needn't show every extreme that they name: `land_mask`: 1 marks an ocean block, 0 a land block; some blocks of every device row are ocean. `barotropic_block_map`: entry d * 3 + s of device row i names the block held in slot s of device d of that row as (gx index of its home device) * 4 + (its block index on that device), or -1 for an empty slot; every ocean block of the row appears exactly once and no land block appears; the device holding a block is its home device or one of the two next to it along gx, periodically; some device holds 3 blocks.
All inputs are finite; a program needn't handle non-finite values.
Results may differ from a plain program's by a relative error of at most 0.0003.
Values may be sent and summed in bfloat16 or wider, within the bound.
A program may use at most 64 MiB of HBM per device.

v0:
```python
import math

import jax
import jax.numpy as jnp
from jax import lax
from jax.sharding import PartitionSpec as P

ITERS = 2


diffusivity = 0.1
flux_gain = 0.5


def extended(cells, sides, width):
    for axis, dim in sides:
        count = lax.axis_size(axis)
        head = lax.slice_in_dim(cells, 0, width, axis=dim)
        tail = lax.slice_in_dim(cells, cells.shape[dim] - width, cells.shape[dim], axis=dim)
        cells = jnp.concatenate(
            [
                lax.ppermute(tail, axis, [(i, (i + 1) % count) for i in range(count)]),
                cells,
                lax.ppermute(head, axis, [((i + 1) % count, i) for i in range(count)]),
            ],
            axis=dim,
        )
    return cells


def upwind(flow_speed, behind, centre, forward, beyond, face_mask):
    centred = (7.0 * (centre + forward) - behind - beyond) / 12.0
    curved = (3.0 * (centre - forward) + beyond - behind) / 12.0
    return face_mask * (
        flow_speed * centred - jnp.abs(flow_speed) * curved - diffusivity * (forward - centre)
    )


def implicit_mix(provisional, vert_diff):
    levels = provisional.shape[1]
    zero_plane = jnp.zeros_like(vert_diff[0])
    cprime = []
    dprime = []
    for level_index in range(levels):
        lower_coef = vert_diff[level_index - 1] if level_index > 0 else zero_plane
        upper_coef = vert_diff[level_index] if level_index < levels - 1 else zero_plane
        centre = 1.0 + lower_coef + upper_coef
        if level_index == 0:
            divisor = centre
            solved = provisional[:, 0] / divisor
        else:
            divisor = centre + lower_coef * cprime[-1]
            solved = (provisional[:, level_index] + lower_coef * dprime[-1]) / divisor
        cprime.append(-upper_coef / divisor)
        dprime.append(solved)
    result = [dprime[-1]]
    for level_index in range(levels - 2, -1, -1):
        result.append(dprime[level_index] - cprime[level_index] * result[-1])
    return jnp.stack(result[::-1], axis=1)


def close_poles(padded, rim_width):
    gy_index = lax.axis_index("gy")
    gy_count = lax.axis_size("gy")
    height = padded.shape[-2]
    row_index = lax.broadcasted_iota(jnp.int32, (height, 1), 0)
    inside = ((row_index >= rim_width) | (gy_index > 0)) & (
        (row_index < height - rim_width) | (gy_index < gy_count - 1)
    )
    return jnp.where(inside, padded, 0.0)


def stencil(padded, diagonal, east_face, west_face, north_face, south_face):
    centre = padded[..., 1:-1, 1:-1]
    return (
        diagonal * centre
        - east_face * padded[..., 1:-1, 2:]
        - west_face * padded[..., 1:-1, :-2]
        - north_face * padded[..., 2:, 1:-1]
        - south_face * padded[..., :-2, 1:-1]
    )


def slot_select(barotropic_block_map, blocks_dev):
    gx_index = lax.axis_index("gx")
    gx_count = lax.axis_size("gx")
    slot_count = barotropic_block_map.shape[1] // gx_count
    held_blocks = lax.dynamic_slice_in_dim(
        barotropic_block_map[0], gx_index * slot_count, slot_count
    )
    source_column = jnp.floor_divide(held_blocks, blocks_dev)
    offset = jnp.mod(source_column - gx_index + 1, gx_count)
    target = offset * blocks_dev + jnp.mod(held_blocks, blocks_dev)
    column = lax.broadcasted_iota(jnp.int32, (slot_count, 3 * blocks_dev), 1)
    chosen = (column == target[:, None]) & (held_blocks[:, None] >= 0)
    return jnp.where(chosen, 1.0, 0.0).astype(jnp.float32)


def total_one(device_local_value):
    return lax.psum(device_local_value, ("gy", "gx"))


def conjugate(right_side, inverse, apply_op, inner_sum):
    solution = jnp.zeros_like(right_side)
    residual = right_side
    precond = inverse * residual
    direction = precond
    rho_now = total_one(inner_sum(residual, precond))
    for repeat in range(ITERS):
        image_field = apply_op(direction)
        step_size = rho_now / total_one(inner_sum(direction, image_field))
        solution = solution + step_size * direction
        residual = residual - step_size * image_field
        if repeat + 1 < ITERS:
            precond = inverse * residual
            rho_next = total_one(inner_sum(residual, precond))
            direction = precond + rho_next / rho_now * direction
            rho_now = rho_next
    return (solution, residual)


def on_device(
    atm_flux,
    remap_source,
    remap_weight,
    tracers,
    velocity,
    vert_diff,
    ocean_depth,
    surface_term,
    land_mask,
    barotropic_block_map,
):
    tracer_count, levels, tile_rows, tile_cols = tracers.shape
    blocks_dev = land_mask.shape[0]
    block_rows = tile_rows // blocks_dev
    cell_mask = jnp.broadcast_to(
        jnp.repeat(land_mask[:, 0].astype(jnp.float32), block_rows)[:, None], (tile_rows, tile_cols)
    )
    atm_near = extended(atm_flux, (("gx", 1),), atm_flux.shape[1])
    picked = atm_near[0][remap_source[:, 0, :]]
    surface_flux = jnp.einsum(
        "rkca,rkfa->frc", remap_weight[:, 0], picked, preferred_element_type=jnp.float32
    )
    masked = tracers * cell_mask
    speed_planes = velocity.reshape(2 * levels, tile_rows, tile_cols)
    stacked = jnp.concatenate(
        [
            masked.reshape(tracer_count * levels, tile_rows, tile_cols),
            speed_planes,
            cell_mask[None],
            ocean_depth[None],
        ],
        axis=0,
    )
    padded = extended(stacked, (("gy", 1), ("gx", 2)), 2)
    padded = close_poles(padded, 2)
    tracer_ext = padded[: tracer_count * levels].reshape(
        tracer_count, levels, tile_rows + 4, tile_cols + 4
    )
    coef_ext = padded[tracer_count * levels :, 1:-1, 1:-1]
    east_speed = coef_ext[:levels]
    north_speed = coef_ext[levels : 2 * levels]
    mask_ext = coef_ext[2 * levels]
    depth_ext = coef_ext[2 * levels + 1]
    east_open = (
        mask_ext[1 : tile_rows + 1, 0 : tile_cols + 1]
        * mask_ext[1 : tile_rows + 1, 1 : tile_cols + 2]
    )
    east_flux = upwind(
        east_speed[:, 1 : tile_rows + 1, 0 : tile_cols + 1],
        tracer_ext[..., 2 : tile_rows + 2, 0 : tile_cols + 1],
        tracer_ext[..., 2 : tile_rows + 2, 1 : tile_cols + 2],
        tracer_ext[..., 2 : tile_rows + 2, 2 : tile_cols + 3],
        tracer_ext[..., 2 : tile_rows + 2, 3 : tile_cols + 4],
        east_open,
    )
    north_open = (
        mask_ext[0 : tile_rows + 1, 1 : tile_cols + 1]
        * mask_ext[1 : tile_rows + 2, 1 : tile_cols + 1]
    )
    north_flux = upwind(
        north_speed[:, 0 : tile_rows + 1, 1 : tile_cols + 1],
        tracer_ext[..., 0 : tile_rows + 1, 2 : tile_cols + 2],
        tracer_ext[..., 1 : tile_rows + 2, 2 : tile_cols + 2],
        tracer_ext[..., 2 : tile_rows + 3, 2 : tile_cols + 2],
        tracer_ext[..., 3 : tile_rows + 4, 2 : tile_cols + 2],
        north_open,
    )
    provisional = cell_mask * (
        masked
        - (east_flux[..., 1:] - east_flux[..., :-1])
        - (north_flux[..., 1:, :] - north_flux[..., :-1, :])
    )
    provisional = provisional.at[:, 0].add(flux_gain * (cell_mask * surface_flux))
    new_tracers = implicit_mix(provisional, vert_diff)
    forcing = (
        cell_mask
        * jnp.sum(new_tracers[0] - new_tracers[1], axis=0)
        * (1.0 / math.sqrt(2.0 * levels))
    )
    east_ext = (
        mask_ext[1:-1, :-1]
        * mask_ext[1:-1, 1:]
        * (depth_ext[1:-1, :-1] + depth_ext[1:-1, 1:])
        * 0.5
    )
    north_ext = (
        mask_ext[:-1, 1:-1]
        * mask_ext[1:, 1:-1]
        * (depth_ext[:-1, 1:-1] + depth_ext[1:, 1:-1])
        * 0.5
    )
    east_weight = east_ext[:, 1:]
    west_weight = east_ext[:, :-1]
    north_weight = north_ext[1:]
    south_weight = north_ext[:-1]
    diagonal = (
        cell_mask * surface_term
        + (1.0 - cell_mask)
        + east_weight
        + west_weight
        + north_weight
        + south_weight
    )
    inverse = 1.0 / diagonal
    chooser = slot_select(barotropic_block_map, blocks_dev)

    def apply_home(field):
        field_pad = extended(field, (("gy", 0), ("gx", 1)), 1)
        field_pad = close_poles(field_pad, 1)
        return stencil(field_pad, diagonal, east_weight, west_weight, north_weight, south_weight)

    def inner_home(first_term, second_term):
        return jnp.sum(first_term * second_term)

    solution, residual = conjugate(forcing, inverse, apply_home, inner_home)
    results = jnp.stack([solution, residual]).reshape(2, blocks_dev, block_rows, tile_cols)
    nearby = extended(results, (("gx", 1),), blocks_dev)
    placed = jnp.einsum("sj,fjrc->fsrc", chooser, nearby, precision=lax.Precision.HIGHEST)
    sea_level = placed[0][None]
    barotropic_slot_residual = placed[1][None]
    return (new_tracers, sea_level, barotropic_slot_residual)


def solution(mesh):
    return jax.shard_map(
        on_device,
        mesh=mesh,
        in_specs=(
            P("gy", "gx", None, None),
            P("gy", "gx", None),
            P("gy", "gx", None, None, None),
            P(None, None, "gy", "gx"),
            P(None, None, "gy", "gx"),
            P(None, "gy", "gx"),
            P("gy", "gx"),
            P("gy", "gx"),
            P("gy", "gx"),
            P("gy", None),
        ),
        out_specs=(P(None, None, "gy", "gx"), P("gy", "gx", None, None), P("gy", "gx", None, None)),
        check_vma=False,
    )
```

profile of v0, /device:TPU:1, one launch (start us, length us, event | category | flops | bytes accessed | tf_op | source)
XLA Modules:
  0.0 489.0 jit_solution(17728222502305708406)
XLA Ops:
  0.6 4.1 collective-permute-start.4
  4.7 6.1 %collective-permute-start.5 = (bf16[1,2,2,128]{3,2,1,0:T(2,128)(2,1)}, bf16[1,2,2,128]{3,2,1,0:T(2,128)(2,1)}, u32[]{:S(2)}, u32[]{:S(2)}) collective-permute-start(bf16[1,2,2,128]{3,2,1,0:T(2,128)(2,1)} %param.12), channel_id=1, source_target_pairs={{1,0},{2,1},{3,2},{4,3},{5,4},{6,5},{7,6},{8,7},{9,8},{10,9},{11,1... | collective-permute-start | bytes 3080 | tf_op jit(solution)/shard_map/ppermute | solution.py:24
  11.7 2.2 copy_multiply_fusion
  15.0 2.9 collective-permute-start
  17.9 3.0 collective-permute-start.1
  23.9 1.4 fusion.107
  25.3 1.4 fusion.109
  26.6 1.4 fusion.111
  28.0 1.4 fusion.113
  29.4 1.4 fusion.115
  51.7 1.6 fusion.117
  53.4 1.5 fusion.119
  54.9 1.4 fusion.121
  56.3 1.4 fusion.123
  57.7 1.4 fusion.125
  59.1 1.4 fusion.127
  69.6 1.4 pad_maximum_fusion
  71.0 3.6 fusion.163
  74.6 2.9 copy.58
  77.4 2.9 copy.59
  80.3 1.9 collective-permute-start.3
  82.2 3.5 collective-permute-start.2
  87.7 2.9 collective-permute-done.2
  90.6 2.9 copy.60
  93.6 3.0 copy.61
  96.6 11.5 %maximum_select_fusion = f32[250,20,132]{2,1,0:T(8,128)S(1)} fusion(f32[250,20,2]{2,1,0:T(8,128)} %copy.61, f32[250,2,128]{2,1,0:T(2,128)} %collective-permute-done.1, f32[1,16,128]{2,1,0:T(8,128)S(1)} %bitcast.1091, f32[1,16,128]{2,1,0:T(8,128)S(1)} %broadcast_in_dim_broadcast_in_dim.2, f32[124,16,128]{2,1,0:T(8,128)S(1)} %bitcast.1080, ...), kind=kLoop, calls=%fused_computation.1 | loop fusion | flops 5280000 | bytes 5280020 | tf_op jit(solution)/shard_map/jit(_where)/select_n | solution.py:70
  110.7 1.6 slice_multiply_fusion
  112.5 3.3 fusion.165
  115.8 1.9 fusion.164
  117.7 5.0 %subtract_multiply_fusion.1 = f32[2,62,17,128]{3,0,2,1:T(2,128)S(1)} fusion(f32[2,62,17,128]{3,2,1,0:T(8,128)} %get-tuple-element.244, f32[2,62,17,128]{3,2,1,0:T(8,128)S(1)} %get-tuple-element.242, f32[2,62,17,128]{3,2,1,0:T(8,128)} %get-tuple-element.243, f32[2,62,17,128]{3,2,1,0:T(8,128)S(1)} %get-tuple-element.241, ...), kind=kLoop, calls=%fused_computation.10 | loop fusion | flops 4047360 | bytes 6484480 | tf_op jit(solution)/shard_map/mul | solution.py:34
  122.7 10.8 %subtract_multiply_fusion = f32[2,62,16,129]{3,0,2,1:T(2,128)S(1)} fusion(f32[2,62,16,129]{3,2,1,0:T(8,128)S(1)} %get-tuple-element.238, f32[2,62,16,129]{3,2,1,0:T(8,128)S(1)} %get-tuple-element.239, f32[2,62,16,129]{3,2,1,0:T(8,128)S(1)} %get-tuple-element.240, f32[2,62,16,129]{3,2,1,0:T(8,128)S(1)} %get-tuple-element.237, f32[62,16,129]{2,1,0:T(8,128)S(1)} %copy-done.5, ...), kind=kLoop, calls=%fused_computation.3 | loop fusion | flops 3839040 | bytes 6150720 | tf_op jit(solution)/shard_map/mul | solution.py:34
  133.6 1.8 fusion.6
  135.8 2.0 add_divide_fusion.3
  138.2 2.3 fusion.20
  140.8 2.1 constant_dynamic-update-slice_fusion.61
  145.5 1.9 collective-permute-start.6
  147.4 4.2 collective-permute-start.7
  152.5 1.9 collective-permute-start.8
  154.4 6.7 %collective-permute-start.9 = (f32[18,1]{1,0:T(8,128)S(1)}, f32[18,1]{1,0:T(8,128)S(1)}, u32[]{:S(2)}, u32[]{:S(2)}) collective-permute-start(f32[18,1]{1,0:T(8,128)S(1)} %get-tuple-element.335), channel_id=1, source_target_pairs={{1,0},{2,1},{3,2},{4,3},{5,4},{6,5},{7,6},{8,7},{9,8},{10,9},{11,1... | collective-permute-start | bytes 224 | tf_op jit(solution)/shard_map/ppermute | solution.py:24
  162.7 102.1 %all-reduce = (f32[]{:T(128)}, f32[]{:T(128)}) all-reduce(f32[]{:T(128)} %get-tuple-element.28, f32[]{:T(128)} %get-tuple-element.27), channel_id=1, replica_groups=mesh['gy'=16,'gx'=32] {'gy','gx'}, use_global_device_ids=true, to_apply=%region_2.3 | all-reduce | flops 2 | bytes 16 | tf_op jit(solution)/shard_map/psum | solution.py:100
  266.8 94.3 %psum.30 = f32[]{:T(128)} all-reduce(f32[]{:T(128)} %get-tuple-element.33), channel_id=1, replica_groups=mesh['gy'=16,'gx'=32] {'gy','gx'}, use_global_device_ids=true, to_apply=%region_6.7 | all-reduce | flops 1 | bytes 8 | tf_op jit(solution)/shard_map/psum | solution.py:100
  363.8 2.0 collective-permute-done.11
  365.9 3.7 collective-permute-start.12
  369.6 4.9 %collective-permute-start.13 = (f32[18,1]{1,0:T(8,128)S(1)}, f32[18,1]{1,0:T(8,128)S(1)}, u32[]{:S(2)}, u32[]{:S(2)}) collective-permute-start(f32[18,1]{1,0:T(8,128)S(1)} %get-tuple-element.333), channel_id=1, source_target_pairs={{1,0},{2,1},{3,2},{4,3},{5,4},{6,5},{7,6},{8,7},{9,8},{10,9},{11,1... | collective-permute-start | bytes 224 | tf_op jit(solution)/shard_map/ppermute | solution.py:24
  376.1 100.3 %psum.31 = f32[]{:T(128)} all-reduce(f32[]{:T(128)} %get-tuple-element.31), channel_id=1, replica_groups=mesh['gy'=16,'gx'=32] {'gy','gx'}, use_global_device_ids=true, to_apply=%region_8.9 | all-reduce | flops 1 | bytes 8 | tf_op jit(solution)/shard_map/psum | solution.py:100
  477.8 1.9 collective-permute-start.15
  479.7 3.4 collective-permute-start.14
  484.2 3.3 collective-permute-done.14
  (403 shorter events, 50.6 us)
Async XLA Ops:
  0.6 134.8 %copy-start = (bf16[16,1,2,128,128]{4,3,2,1,0:T(8,128)(2,1)S(1)}, bf16[16,1,2,128,128]{4,3,2,1,0:T(8,128)(2,1)}, u32[]{:S(2)}) copy-start(bf16[16,1,2,128,128]{4,3,2,1,0:T(8,128)(2,1)} %param.14) | copy-start | bytes 3145732
  0.6 85.2 %collective-permute-start.4 = (bf16[1,2,2,128]{3,2,1,0:T(2,128)(2,1)}, bf16[1,2,2,128]{3,2,1,0:T(2,128)(2,1)}, u32[]{:S(2)}, u32[]{:S(2)}) collective-permute-start(bf16[1,2,2,128]{3,2,1,0:T(2,128)(2,1)} %param.12), channel_id=1, source_target_pairs={{0,1},{1,2},{2,3},{3,4},{4,5},{5,6},{6,7},{7,8},{8,9},{9,10},{10,1... | collective-permute-start | bytes 3080 | tf_op jit(solution)/shard_map/ppermute | solution.py:22
  4.7 81.1 %collective-permute-start.5 = (bf16[1,2,2,128]{3,2,1,0:T(2,128)(2,1)}, bf16[1,2,2,128]{3,2,1,0:T(2,128)(2,1)}, u32[]{:S(2)}, u32[]{:S(2)}) collective-permute-start(bf16[1,2,2,128]{3,2,1,0:T(2,128)(2,1)} %param.12), channel_id=1, source_target_pairs={{1,0},{2,1},{3,2},{4,3},{5,4},{6,5},{7,6},{8,7},{9,8},{10,9},{11,1... | collective-permute-start | bytes 3080 | tf_op jit(solution)/shard_map/ppermute | solution.py:24
  11.6 9.3 %copy-start.117 = (f32[16]{0:T(128)}, f32[16]{0:T(128)S(1)}, u32[]{:S(2)}) copy-start(f32[16]{0:T(128)S(1)} %broadcast_in_dim_reshape.3) | copy-start | bytes 196
  13.8 9.3 %copy-start.121 = (s32[16,1,2]{0,2,1:T(2,128)S(1)}, s32[16,1,2]{0,2,1:T(2,128)}, u32[]{:S(2)}) copy-start(s32[16,1,2]{0,2,1:T(2,128)} %param.13) | copy-start | bytes 388
  15.0 54.3 %collective-permute-start = (f32[250,2,128]{2,1,0:T(2,128)}, f32[250,2,128]{2,1,0:T(2,128)S(1)}, u32[]{:S(2)}, u32[]{:S(2)}) collective-permute-start(f32[250,2,128]{2,1,0:T(2,128)} %get-tuple-element.245), channel_id=1, source_target_pairs={{0,32},{32,64},{64,96},{96,128},{128,160},{160,192},{192,224},{224... | collective-permute-start | bytes 768008 | tf_op jit(solution)/shard_map/ppermute | solution.py:22
  17.9 51.7 %collective-permute-start.1 = (f32[250,2,128]{2,1,0:T(2,128)}, f32[250,2,128]{2,1,0:T(2,128)}, u32[]{:S(2)}, u32[]{:S(2)}) collective-permute-start(f32[250,2,128]{2,1,0:T(2,128)} %get-tuple-element.246), channel_id=1, source_target_pairs={{32,0},{64,32},{96,64},{128,96},{160,128},{192,160},{224,192},{256... | collective-permute-start | bytes 768008 | tf_op jit(solution)/shard_map/ppermute | solution.py:24
  23.3 37.1 %copy-start.3 = (f32[61,16,128]{2,1,0:T(8,128)S(1)}, f32[61,16,128]{2,1,0:T(8,128)}, u32[]{:S(2)}) copy-start(f32[61,16,128]{2,1,0:T(8,128)} %param.17) | copy-start | bytes 1499140
  25.3 44.0 %copy-start.73 = (f32[1,16,128]{2,1,0:T(8,128)}, f32[1,16,128]{2,1,0:T(8,128)S(1)}, u32[]{:S(2)}) copy-start(f32[1,16,128]{2,1,0:T(8,128)S(1)} %get-tuple-element.94) | copy-start | bytes 24580
  25.3 45.7 %copy-start.71 = (f32[1,16,128]{2,1,0:T(8,128)}, f32[1,16,128]{2,1,0:T(8,128)S(1)}, u32[]{:S(2)}) copy-start(f32[1,16,128]{2,1,0:T(8,128)S(1)} %get-tuple-element.93) | copy-start | bytes 24580
  26.6 24.3 %copy-start.75 = (f32[1,16,128]{2,1,0:T(8,128)}, f32[1,16,128]{2,1,0:T(8,128)S(1)}, u32[]{:S(2)}) copy-start(f32[1,16,128]{2,1,0:T(8,128)S(1)} %get-tuple-element.96) | copy-start | bytes 24580
  26.6 42.6 %copy-start.77 = (f32[1,16,128]{2,1,0:T(8,128)}, f32[1,16,128]{2,1,0:T(8,128)S(1)}, u32[]{:S(2)}) copy-start(f32[1,16,128]{2,1,0:T(8,128)S(1)} %get-tuple-element.97) | copy-start | bytes 24580
  28.0 25.3 %copy-start.78 = (f32[1,16,128]{2,1,0:T(8,128)}, f32[1,16,128]{2,1,0:T(8,128)S(1)}, u32[]{:S(2)}) copy-start(f32[1,16,128]{2,1,0:T(8,128)S(1)} %get-tuple-element.99) | copy-start | bytes 24580
  28.0 36.8 %copy-start.79 = (f32[1,16,128]{2,1,0:T(8,128)}, f32[1,16,128]{2,1,0:T(8,128)S(1)}, u32[]{:S(2)}) copy-start(f32[1,16,128]{2,1,0:T(8,128)S(1)} %get-tuple-element.100) | copy-start | bytes 24580
  29.4 24.0 %copy-start.80 = (f32[1,16,128]{2,1,0:T(8,128)}, f32[1,16,128]{2,1,0:T(8,128)S(1)}, u32[]{:S(2)}) copy-start(f32[1,16,128]{2,1,0:T(8,128)S(1)} %get-tuple-element.102) | copy-start | bytes 24580
  29.4 39.9 %copy-start.81 = (f32[1,16,128]{2,1,0:T(8,128)}, f32[1,16,128]{2,1,0:T(8,128)S(1)}, u32[]{:S(2)}) copy-start(f32[1,16,128]{2,1,0:T(8,128)S(1)} %get-tuple-element.103) | copy-start | bytes 24580
  30.7 22.6 %copy-start.82 = (f32[1,16,128]{2,1,0:T(8,128)}, f32[1,16,128]{2,1,0:T(8,128)S(1)}, u32[]{:S(2)}) copy-start(f32[1,16,128]{2,1,0:T(8,128)S(1)} %get-tuple-element.105) | copy-start | bytes 24580
  30.7 38.6 %copy-start.83 = (f32[1,16,128]{2,1,0:T(8,128)}, f32[1,16,128]{2,1,0:T(8,128)S(1)}, u32[]{:S(2)}) copy-start(f32[1,16,128]{2,1,0:T(8,128)S(1)} %get-tuple-element.106) | copy-start | bytes 24580
  41.4 8.8 %copy-start.7 = (f32[16,128]{1,0:T(8,128)}, f32[16,128]{1,0:T(8,128)S(1)}, u32[]{:S(2)}) copy-start(f32[16,128]{1,0:T(8,128)S(1)} %get-tuple-element.172) | copy-start | bytes 24580
  44.1 21.9 %copy-start.9 = (f32[16,128]{1,0:T(8,128)}, f32[16,128]{1,0:T(8,128)S(1)}, u32[]{:S(2)}) copy-start(f32[16,128]{1,0:T(8,128)S(1)} %get-tuple-element.176) | copy-start | bytes 24580
  46.8 19.3 %copy-start.11 = (f32[16,128]{1,0:T(8,128)}, f32[16,128]{1,0:T(8,128)S(1)}, u32[]{:S(2)}) copy-start(f32[16,128]{1,0:T(8,128)S(1)} %get-tuple-element.180) | copy-start | bytes 24580
  53.3 16.0 %copy-start.84 = (f32[1,16,128]{2,1,0:T(8,128)}, f32[1,16,128]{2,1,0:T(8,128)S(1)}, u32[]{:S(2)}) copy-start(f32[1,16,128]{2,1,0:T(8,128)S(1)} %get-tuple-element.108) | copy-start | bytes 24580
  53.3 16.0 %copy-start.106 = (f32[1,16,128]{2,1,0:T(8,128)}, f32[1,16,128]{2,1,0:T(8,128)S(1)}, u32[]{:S(2)}) copy-start(f32[1,16,128]{2,1,0:T(8,128)S(1)} %get-tuple-element.109) | copy-start | bytes 24580
  54.9 14.4 %copy-start.107 = (f32[1,16,128]{2,1,0:T(8,128)}, f32[1,16,128]{2,1,0:T(8,128)S(1)}, u32[]{:S(2)}) copy-start(f32[1,16,128]{2,1,0:T(8,128)S(1)} %get-tuple-element.112) | copy-start | bytes 24580
  56.3 13.0 %copy-start.114 = (f32[1,16,128]{2,1,0:T(8,128)}, f32[1,16,128]{2,1,0:T(8,128)S(1)}, u32[]{:S(2)}) copy-start(f32[1,16,128]{2,1,0:T(8,128)S(1)} %get-tuple-element.115) | copy-start | bytes 24580
  57.7 11.6 %copy-start.85 = (f32[1,16,128]{2,1,0:T(8,128)}, f32[1,16,128]{2,1,0:T(8,128)S(1)}, u32[]{:S(2)}) copy-start(f32[1,16,128]{2,1,0:T(8,128)S(1)} %get-tuple-element.117) | copy-start | bytes 24580
  57.7 11.7 %copy-start.108 = (f32[1,16,128]{2,1,0:T(8,128)}, f32[1,16,128]{2,1,0:T(8,128)S(1)}, u32[]{:S(2)}) copy-start(f32[1,16,128]{2,1,0:T(8,128)S(1)} %get-tuple-element.118) | copy-start | bytes 24580
  59.1 10.3 %copy-start.86 = (f32[1,16,128]{2,1,0:T(8,128)}, f32[1,16,128]{2,1,0:T(8,128)S(1)}, u32[]{:S(2)}) copy-start(f32[1,16,128]{2,1,0:T(8,128)S(1)} %get-tuple-element.120) | copy-start | bytes 24580
  59.1 10.3 %copy-start.109 = (f32[1,16,128]{2,1,0:T(8,128)}, f32[1,16,128]{2,1,0:T(8,128)S(1)}, u32[]{:S(2)}) copy-start(f32[1,16,128]{2,1,0:T(8,128)S(1)} %get-tuple-element.121) | copy-start | bytes 24580
  60.5 8.9 %copy-start.87 = (f32[1,16,128]{2,1,0:T(8,128)}, f32[1,16,128]{2,1,0:T(8,128)S(1)}, u32[]{:S(2)}) copy-start(f32[1,16,128]{2,1,0:T(8,128)S(1)} %get-tuple-element.123) | copy-start | bytes 24580
  60.5 8.9 %copy-start.88 = (f32[1,16,128]{2,1,0:T(8,128)}, f32[1,16,128]{2,1,0:T(8,128)S(1)}, u32[]{:S(2)}) copy-start(f32[1,16,128]{2,1,0:T(8,128)S(1)} %get-tuple-element.124) | copy-start | bytes 24580
  77.4 9.1 %copy-start.116 = (s32[1024]{0:T(1024)S(1)}, s32[1024]{0:T(1024)}, u32[]{:S(2)}) copy-start(s32[1024]{0:T(1024)} %pad_clamp_fusion) | copy-start | bytes 12292
  80.3 13.2 %collective-permute-start.3 = (f32[250,20,2]{0,2,1:T(2,128)}, f32[250,20,2]{0,2,1:T(2,128)}, u32[]{:S(2)}, u32[]{:S(2)}) collective-permute-start(f32[250,20,2]{0,2,1:T(2,128)} %copy.59), channel_id=1, source_target_pairs={{1,0},{2,1},{3,2},{4,3},{5,4},{6,5},{7,6},{8,7},{9,8},{10,9},{11,1... | collective-permute-start | bytes 120008 | tf_op jit(solution)/shard_map/ppermute | solution.py:24
  82.2 8.4 %collective-permute-start.2 = (f32[250,20,2]{0,2,1:T(2,128)}, f32[250,20,2]{0,2,1:T(2,128)}, u32[]{:S(2)}, u32[]{:S(2)}) collective-permute-start(f32[250,20,2]{0,2,1:T(2,128)} %copy.58), channel_id=1, source_target_pairs={{0,1},{1,2},{2,3},{3,4},{4,5},{5,6},{6,7},{7,8},{8,9},{9,10},{10,1... | collective-permute-start | bytes 120008 | tf_op jit(solution)/shard_map/ppermute | solution.py:22
  122.7 10.9 %copy-start.6 = (f32[2,62,16,128]{3,2,1,0:T(8,128)S(1)}, f32[2,62,16,128]{3,2,1,0:T(8,128)}, u32[]{:S(2)}) copy-start(f32[2,62,16,128]{3,2,1,0:T(8,128)} %param.15) | copy-start | bytes 3047428
  122.7 10.9 %copy-start.118 = (f32[16]{0:T(128)S(1)}, f32[16]{0:T(128)}, u32[]{:S(2)}) copy-start(f32[16]{0:T(128)} %copy-done.117) | copy-start | bytes 196
  143.3 18.6 %copy-start.120 = (pred[18]{0:T(512)(128)(4,1)S(1)}, pred[18]{0:T(512)(128)(4,1)}, u32[]{:S(2)}) copy-start(pred[18]{0:T(512)(128)(4,1)} %or_and_fusion) | copy-start | bytes 58
  143.5 219.7 %copy-start.125 = (s32[1,96]{1,0:T(1,128)S(1)}, s32[1,96]{1,0:T(1,128)}, u32[]{:S(2)}) copy-start(s32[1,96]{1,0:T(1,128)} %param.21) | copy-start | bytes 1156
  145.5 6.7 %collective-permute-start.6 = (f32[1,128]{1,0:T(1,128)S(1)}, f32[1,128]{1,0:T(1,128)S(1)}, u32[]{:S(2)}, u32[]{:S(2)}) collective-permute-start(f32[1,128]{1,0:T(1,128)S(1)} %get-tuple-element.338), channel_id=1, source_target_pairs={{0,32},{32,64},{64,96},{96,128},{128,160},{160,192},{192,224},{224... | collective-permute-start | bytes 1544 | tf_op jit(solution)/shard_map/ppermute | solution.py:22
  147.4 5.0 %collective-permute-start.7 = (f32[1,128]{1,0:T(1,128)S(1)}, f32[1,128]{1,0:T(1,128)S(1)}, u32[]{:S(2)}, u32[]{:S(2)}) collective-permute-start(f32[1,128]{1,0:T(1,128)S(1)} %get-tuple-element.339), channel_id=1, source_target_pairs={{32,0},{64,32},{96,64},{128,96},{160,128},{192,160},{224,192},{256... | collective-permute-start | bytes 1544 | tf_op jit(solution)/shard_map/ppermute | solution.py:24
  152.5 8.6 %collective-permute-start.8 = (f32[18,1]{1,0:T(8,128)S(1)}, f32[18,1]{1,0:T(8,128)S(1)}, u32[]{:S(2)}, u32[]{:S(2)}) collective-permute-start(f32[18,1]{1,0:T(8,128)S(1)} %get-tuple-element.334), channel_id=1, source_target_pairs={{0,1},{1,2},{2,3},{3,4},{4,5},{5,6},{6,7},{7,8},{8,9},{9,10},{10,1... | collective-permute-start | bytes 224 | tf_op jit(solution)/shard_map/ppermute | solution.py:22
  154.4 7.5 %collective-permute-start.9 = (f32[18,1]{1,0:T(8,128)S(1)}, f32[18,1]{1,0:T(8,128)S(1)}, u32[]{:S(2)}, u32[]{:S(2)}) collective-permute-start(f32[18,1]{1,0:T(8,128)S(1)} %get-tuple-element.335), channel_id=1, source_target_pairs={{1,0},{2,1},{3,2},{4,3},{5,4},{6,5},{7,6},{8,7},{9,8},{10,9},{11,1... | collective-permute-start | bytes 224 | tf_op jit(solution)/shard_map/ppermute | solution.py:24
  362.5 1.3 collective-permute-start.10
  362.9 3.0 collective-permute-start.11
  365.9 8.6 %collective-permute-start.12 = (f32[18,1]{1,0:T(8,128)S(1)}, f32[18,1]{1,0:T(8,128)S(1)}, u32[]{:S(2)}, u32[]{:S(2)}) collective-permute-start(f32[18,1]{1,0:T(8,128)S(1)} %get-tuple-element.332), channel_id=1, source_target_pairs={{0,1},{1,2},{2,3},{3,4},{4,5},{5,6},{6,7},{7,8},{8,9},{9,10},{10,1... | collective-permute-start | bytes 224 | tf_op jit(solution)/shard_map/ppermute | solution.py:22
  369.6 5.7 %collective-permute-start.13 = (f32[18,1]{1,0:T(8,128)S(1)}, f32[18,1]{1,0:T(8,128)S(1)}, u32[]{:S(2)}, u32[]{:S(2)}) collective-permute-start(f32[18,1]{1,0:T(8,128)S(1)} %get-tuple-element.333), channel_id=1, source_target_pairs={{1,0},{2,1},{3,2},{4,3},{5,4},{6,5},{7,6},{8,7},{9,8},{10,9},{11,1... | collective-permute-start | bytes 224 | tf_op jit(solution)/shard_map/ppermute | solution.py:24
  477.8 6.4 %collective-permute-start.15 = (f32[2,4,4,128]{3,1,2,0:T(4,128)S(1)}, f32[2,4,4,128]{3,1,2,0:T(4,128)S(1)}, u32[]{:S(2)}, u32[]{:S(2)}) collective-permute-start(f32[2,4,4,128]{3,1,2,0:T(4,128)S(1)} %constant_dynamic-update-slice_fusion.62), channel_id=1, source_target_pairs={{1,0},{2,1},{3,2},{4,3},{5,4},{6,5},{7,6},{8,7},{9,8},{10,9},{11,1... | collective-permute-start | bytes 49160 | tf_op jit(solution)/shard_map/ppermute | solution.py:24
  479.7 7.8 %collective-permute-start.14 = (f32[2,4,4,128]{3,1,2,0:T(4,128)S(1)}, f32[2,4,4,128]{3,1,2,0:T(4,128)S(1)}, u32[]{:S(2)}, u32[]{:S(2)}) collective-permute-start(f32[2,4,4,128]{3,1,2,0:T(4,128)S(1)} %constant_dynamic-update-slice_fusion.62), channel_id=1, source_target_pairs={{0,1},{1,2},{2,3},{3,4},{4,5},{5,6},{6,7},{7,8},{8,9},{9,10},{10,1... | collective-permute-start | bytes 49160 | tf_op jit(solution)/shard_map/ppermute | solution.py:22
  (94 other events, 311.8 us)
where the time goes:
time: 493 us; the launch traced here: 489 us
  blocking collectives  297 us (60%)
  other arithmetic  95.6 us (19%)
  starting transfers between devices  50.9 us (10%)
  local copies, waits for them, and re-layouts  25.6 us (5%)
  waiting for transfers between devices  11.2 us (2%)
  between operations  6.72 us (1%)
    psum x3, blocking collectives, total_one(): return lax.psum(device_local_value, ('gy', 'gx'))  297 us
    ppermute x8, starting transfers between devices, extended(): lax.ppermute(head, axis, [((i + 1) % count, i) for i in range(count)])  29.1 us
    mul x23, other arithmetic, implicit_mix(): result.append(dprime[level_index] - cprime[level_index] * result[-1])  23 us
    add x18, other arithmetic, implicit_mix(): divisor = centre + lower_coef * cprime[-1]  21.9 us
    ppermute x8, starting transfers between devices, extended(): lax.ppermute(tail, axis, [(i, (i + 1) % count) for i in range(count)])  21.7 us
    mul x2, other arithmetic, upwind(): face_mask * (flow_speed * centred - jnp.abs(flow_speed) * curved - diffus...  15.8 us
    select_n x3, other arithmetic, close_poles(): return jnp.where(inside, padded, 0.0)  11.7 us
  transfers between devices with their start and end apart: 16, of which 8 were waited for; matrix products, arithmetic and copies ran while one was open for 14% of the time, Pallas kernels for 0%

commit v1 on v0

v1 whole, which is shorter than its diff:
```python
import functools
import math

import jax
import jax.numpy as jnp
from jax import lax
from jax.experimental import pallas as pl
from jax.experimental.pallas import tpu as pltpu
from jax.sharding import PartitionSpec as P

DIFFUSIVITY = 0.1
FLUX_GAIN = 0.5
MESH = pl.DeviceIdType.MESH
GROUP = 8
SIDES = ((0, 1), (0, -1), (1, 0), (-1, 0), (1, 1), (1, -1), (-1, 1), (-1, -1))
META, ATM, EDGE, SEARCH, SLOT, REDUCE = 0, 8, 10, 16, 24, 26
COPIES = REDUCE + 3 * (GROUP - 1)


def flux(speed, behind, centre, forward, beyond, mixing):
    drop = centre - forward
    return (
        speed * (7.0 * (centre + forward) - (behind + beyond))
        - jnp.abs(speed) * (3.0 * drop + (beyond - behind))
        + mixing * drop
    )


def kernel(
    n_gy,
    n_gx,
    source_ref,
    land_ref,
    map_ref,
    atm_ref,
    depth_ref,
    surface_ref,
    weight_hbm,
    tracer_hbm,
    velocity_hbm,
    vert_hbm,
    new_hbm,
    sea_ref,
    slot_ref,
    weight,
    cells,
    east_speed,
    north_speed,
    vert,
    meta_own,
    meta,
    atm_own,
    atm_near,
    to_north,
    to_south,
    from_south,
    from_north,
    speed_north,
    speed_south,
    edge_own,
    edge_near,
    speed_east,
    speed_west,
    west_face,
    surface_flux,
    factor,
    solved,
    search_own,
    search,
    fields,
    fields_near,
    partial,
    gathered,
    placed,
    local_sem,
    send_sem,
    recv_sem,
):
    tracer_count, levels, rows, cols = tracer_hbm.shape
    gy = lax.axis_index("gy")
    gx = lax.axis_index("gx")

    loads = [
        pltpu.make_async_copy(tracer_hbm, cells.at[:, :, 8 : 8 + rows, :], local_sem.at[0]),
        pltpu.make_async_copy(velocity_hbm.at[0], east_speed, local_sem.at[1]),
        pltpu.make_async_copy(
            velocity_hbm.at[1], north_speed.at[:, 8 : 8 + rows, :], local_sem.at[2]
        ),
        pltpu.make_async_copy(weight_hbm, weight, local_sem.at[3]),
        pltpu.make_async_copy(vert_hbm, vert.at[1:levels], local_sem.at[4]),
    ]
    for load in loads:
        load.start()

    def beside(dy, dx):
        return (lax.rem(gy + dy + n_gy, n_gy), lax.rem(gx + dx + n_gx, n_gx))

    inner_gy, inner_gx = n_gy // GROUP, n_gx // GROUP
    core, column = lax.rem(gy, inner_gy), lax.rem(gx, inner_gx)
    flat = core * inner_gx + column

    def partner(stage, k):
        if stage == 0:
            other = lax.rem(flat + k, GROUP)
            return (gy - core + other // inner_gx, gx - column + lax.rem(other, inner_gx))
        if stage == 1:
            return (gy, lax.rem(gx + k * inner_gx, n_gx))
        return (lax.rem(gy + k * inner_gy, n_gy), gx)

    barrier = pltpu.get_barrier_semaphore()
    peers = [beside(dy, dx) for dy, dx in SIDES]
    peers += [partner(stage, k) for stage in range(3) for k in range(1, GROUP)]
    for peer in peers:
        pl.semaphore_signal(barrier, inc=1, device_id=peer, device_id_type=MESH)

    def remote(index, src, dst, device):
        copy = pltpu.make_async_remote_copy(
            src_ref=src,
            dst_ref=dst,
            send_sem=send_sem.at[index],
            recv_sem=recv_sem.at[index],
            device_id=device,
            device_id_type=MESH,
        )
        copy.start()
        return copy

    def sides(first, own, padded):
        lead = (slice(None),) * (len(own.shape) - 2)
        source_rows = {0: slice(0, rows), 1: slice(rows - 8, rows), -1: slice(0, 8)}
        target_rows = {0: slice(8, 8 + rows), 1: slice(0, 8), -1: slice(8 + rows, 16 + rows)}
        target_cols = {
            0: slice(cols, 2 * cols),
            1: slice(0, cols),
            -1: slice(2 * cols, 3 * cols),
        }
        return [
            remote(
                first + k,
                own.at[lead + (source_rows[dy],)],
                padded.at[lead + (target_rows[dy], target_cols[dx])],
                beside(dy, dx),
            )
            for k, (dy, dx) in enumerate(SIDES)
        ]

    row = lax.broadcasted_iota(jnp.int32, (rows, cols), 0)
    lane = lax.broadcasted_iota(jnp.int32, (rows, cols), 1)
    block_rows = rows // land_ref.shape[0]
    mask = jnp.zeros((rows, cols), jnp.float32)
    for block in range(land_ref.shape[0]):
        wet = land_ref[block, 0].astype(jnp.float32)
        mask = jnp.where(row // block_rows == block, wet, mask)
    meta_own[0] = mask
    meta_own[1] = depth_ref[...]
    meta_own[2] = surface_ref[...]
    for k in range(3):
        meta[k, 8 : 8 + rows, cols : 2 * cols] = meta_own[k]
    atm_own[...] = atm_ref[0].astype(jnp.float32)
    blocks_near = atm_own.shape[0]
    atm_near[blocks_near : 2 * blocks_near] = atm_own[...]

    pl.semaphore_wait(barrier, len(peers))
    sent = sides(META, meta_own, meta)
    meta_copies = list(sent)
    atm_copies = [
        remote(ATM, atm_own, atm_near.at[0:blocks_near], beside(0, 1)),
        remote(ATM + 1, atm_own, atm_near.at[2 * blocks_near : 3 * blocks_near], beside(0, -1)),
    ]

    loads[0].wait()
    zero = jnp.zeros((rows, cols), jnp.float32)
    pair = lane // 2

    def pack(level, packed):
        packed = list(packed)
        here = pair == level
        for f in range(tracer_count):
            values = cells[f, level, 8 : 8 + rows, :] * mask
            cells[f, level, 8 : 8 + rows, :] = values
            to_north[f, level] = values[rows - 2 :]
            to_south[f, level] = values[:2]
            packed[2 * f] = jnp.where(here, pltpu.roll(values, 2 * level, 1), packed[2 * f])
            packed[2 * f + 1] = jnp.where(
                here, pltpu.roll(values, lax.rem(2 * level + 2, cols), 1), packed[2 * f + 1]
            )
        return tuple(packed)

    packed = lax.fori_loop(0, levels, pack, (zero,) * (2 * tracer_count), unroll=2)
    for f in range(tracer_count):
        edge_own[0, f] = packed[2 * f]
        edge_own[1, f] = packed[2 * f + 1]
    edge_copies = [
        remote(EDGE, to_north, from_south, beside(1, 0)),
        remote(EDGE + 1, to_south, from_north, beside(-1, 0)),
        remote(EDGE + 2, edge_own.at[0], edge_near.at[0], beside(0, -1)),
        remote(EDGE + 3, edge_own.at[1], edge_near.at[1], beside(0, 1)),
    ]

    loads[1].wait()
    loads[2].wait()

    def pack_speed(level, packed):
        speed_north[pl.ds(level, 1), :] = north_speed[level, 7 + rows : 8 + rows, :]
        return jnp.where(
            pair == level,
            pltpu.roll(east_speed[level], lax.rem(2 * level + 1, cols), 1),
            packed,
        )

    speed_east[...] = lax.fori_loop(0, levels, pack_speed, zero, unroll=2)
    edge_copies += [
        remote(EDGE + 4, speed_north, speed_south, beside(1, 0)),
        remote(EDGE + 5, speed_east, speed_west, beside(0, 1)),
    ]

    loads[3].wait()
    for copy in atm_copies:
        copy.wait_recv()

    def remap(r, carry):
        total = jnp.zeros((tracer_count, cols), jnp.float32)
        for k in range(weight.shape[2]):
            picked = atm_near[source_ref[r, 0, k]].astype(jnp.bfloat16)
            total += lax.dot_general(
                picked,
                weight[r, 0, k],
                (((1,), (1,)), ((), ())),
                preferred_element_type=jnp.float32,
            )
        for f in range(tracer_count):
            surface_flux[f, pl.ds(r, 1), :] = total[f : f + 1]
        return carry

    lax.fori_loop(0, rows, remap, 0, unroll=4)
    for f in range(tracer_count):
        surface_flux[f] = FLUX_GAIN * mask * surface_flux[f]

    for copy in meta_copies:
        copy.wait_recv()
    height, width = search.shape
    wide_row = lax.broadcasted_iota(jnp.int32, (height, width), 0)
    below = jnp.where(gy > 0, 1.0, 0.0)
    above = jnp.where(gy < n_gy - 1, 1.0, 0.0)
    inside = jnp.where(wide_row < 8, below, jnp.where(wide_row >= 8 + rows, above, 1.0))
    wide_mask = meta[0] * inside
    depth = meta[1]

    def next_col(v):
        return pltpu.roll(v, width - 1, 1)

    def last_col(v):
        return pltpu.roll(v, 1, 1)

    def next_row(v):
        return pltpu.roll(v, height - 1, 0)

    def last_row(v):
        return pltpu.roll(v, 1, 0)

    wide_east = wide_mask * next_col(wide_mask)
    wide_north = wide_mask * next_row(wide_mask)
    east_weight = wide_east * (depth + next_col(depth)) * 0.5
    north_weight = wide_north * (depth + next_row(depth)) * 0.5
    west_weight = last_col(east_weight)
    south_weight = last_row(north_weight)
    diagonal = (
        wide_mask * meta[2]
        + (1.0 - wide_mask)
        + east_weight
        + west_weight
        + north_weight
        + south_weight
    )
    inverse = 1.0 / diagonal
    wide_south = last_row(wide_north)
    wide_west = last_col(wide_east)

    def centre(v):
        return v[8 : 8 + rows, cols : 2 * cols]

    east_open = centre(wide_east) * (1.0 / 12.0)
    north_open = centre(wide_north) * (1.0 / 12.0)
    south_open = centre(wide_south) * (1.0 / 12.0)
    west_open = jnp.broadcast_to(centre(wide_west)[:, :1], (rows, cols)) * (1.0 / 12.0)
    mask_south = wide_mask[6:8, cols : 2 * cols]
    mask_north = wide_mask[8 + rows : 10 + rows, cols : 2 * cols]

    for copy in edge_copies:
        copy.wait_recv()

    def place(level, carry):
        for f in range(tracer_count):
            cells[f, level, 6:8, :] = from_south[f, level] * mask_south
            cells[f, level, 8 + rows : 10 + rows, :] = from_north[f, level] * mask_north
        north_speed[level, 7:8, :] = speed_south[pl.ds(level, 1), :]
        return carry

    lax.fori_loop(0, levels, place, 0, unroll=2)
    for f in range(tracer_count):
        behind = edge_near[1, f]
        ahead = edge_own[0, f]
        west_face[f] = flux(
            speed_west[...] * west_open,
            behind,
            pltpu.roll(behind, cols - 1, 1),
            ahead,
            pltpu.roll(ahead, cols - 1, 1),
            (12.0 * DIFFUSIVITY) * west_open,
        )

    loads[4].wait()
    vert[0] = zero
    vert[levels] = zero

    def advected(level):
        along = east_speed[level] * east_open
        across_north = north_speed[level, 8 : 8 + rows, :] * north_open
        across_south = north_speed[level, 7 : 7 + rows, :] * south_open
        twice = 2 * level
        results = []
        for f in range(tracer_count):
            here = cells[f, level, 8 : 8 + rows, :]
            south1 = cells[f, level, 7 : 7 + rows, :]
            south2 = cells[f, level, 6 : 6 + rows, :]
            north1 = cells[f, level, 9 : 9 + rows, :]
            north2 = cells[f, level, 10 : 10 + rows, :]
            right = pltpu.roll(edge_near[0, f], lax.rem(2 * cols - 2 - twice, cols), 1)
            east2 = jnp.where(lane >= cols - 2, right, pltpu.roll(here, cols - 2, 1))
            east1 = jnp.where(
                lane == cols - 1, pltpu.roll(right, 1, 1), pltpu.roll(here, cols - 1, 1)
            )
            west1 = jnp.where(
                lane == 0,
                pltpu.roll(edge_near[1, f], lax.rem(2 * cols - 1 - twice, cols), 1),
                pltpu.roll(here, 1, 1),
            )
            east_flux = flux(along, west1, here, east1, east2, mix_east)
            west_flux = jnp.where(
                lane == 0,
                pltpu.roll(west_face[f], lax.rem(2 * cols - twice, cols), 1),
                pltpu.roll(east_flux, 1, 1),
            )
            north_flux = flux(across_north, south1, here, north1, north2, mix_north)
            south_flux = flux(across_south, south2, south1, here, north1, mix_south)
            results.append(
                mask * (here - (east_flux - west_flux) - (north_flux - south_flux))
            )
        return results

    mix_east = (12.0 * DIFFUSIVITY) * east_open
    mix_north = (12.0 * DIFFUSIVITY) * north_open
    mix_south = (12.0 * DIFFUSIVITY) * south_open

    half = levels // 2

    def eliminate(step, carry):
        top, top_values, bottom, bottom_values = carry
        low, high = step, levels - 1 - step
        share = jnp.where(step == 0, 1.0, 0.0)
        lower, upper = vert[low], vert[low + 1]
        scale = 1.0 / (1.0 + lower + upper + lower * top)
        top = -upper * scale
        factor[low] = top
        provisional = advected(low)
        top_values = tuple(
            (provisional[f] + share * surface_flux[f] + lower * top_values[f]) * scale
            for f in range(tracer_count)
        )
        for f in range(tracer_count):
            solved[f, low] = top_values[f]
        lower, upper = vert[high], vert[high + 1]
        scale = 1.0 / (1.0 + lower + upper + upper * bottom)
        bottom = -lower * scale
        factor[high] = bottom
        provisional = advected(high)
        bottom_values = tuple(
            (provisional[f] + upper * bottom_values[f]) * scale for f in range(tracer_count)
        )
        for f in range(tracer_count):
            solved[f, high] = bottom_values[f]
        return top, top_values, bottom, bottom_values

    none = (zero,) * tracer_count
    top, top_values, bottom, bottom_values = lax.fori_loop(
        0, half, eliminate, (zero, none, zero, none)
    )
    across = 1.0 / (1.0 - top * bottom)
    up, down = [], []
    for f in range(tracer_count):
        upper_value = (top_values[f] - top * bottom_values[f]) * across
        lower_value = bottom_values[f] - bottom * upper_value
        solved[f, half - 1] = upper_value
        solved[f, half] = lower_value
        up.append(upper_value)
        down.append(lower_value)
    total = (up[0] - up[1]) + (down[0] - down[1])

    def substitute(step, carry):
        up, down, total = carry
        low, high = half - 2 - step, half + 1 + step
        up = tuple(solved[f, low] - factor[low] * up[f] for f in range(tracer_count))
        down = tuple(solved[f, high] - factor[high] * down[f] for f in range(tracer_count))
        for f in range(tracer_count):
            solved[f, low] = up[f]
            solved[f, high] = down[f]
        return up, down, total + ((up[0] - up[1]) + (down[0] - down[1]))

    _, _, total = lax.fori_loop(
        0, half - 1, substitute, (tuple(up), tuple(down), total), unroll=2
    )
    store = pltpu.make_async_copy(solved, new_hbm, local_sem.at[5])
    store.start()

    forcing = mask * total * (1.0 / math.sqrt(2.0 * levels))
    first = centre(inverse) * forcing
    search_own[...] = first
    search[8 : 8 + rows, cols : 2 * cols] = first
    search_copies = sides(SEARCH, search_own, search)
    for copy in search_copies:
        copy.wait_recv()

    def operator(v):
        return (
            diagonal * v
            - east_weight * next_col(v)
            - west_weight * last_col(v)
            - north_weight * next_row(v)
            - south_weight * last_row(v)
        )

    wide_image = operator(search[...])
    wide_second = inverse * wide_image
    image = centre(wide_image)
    second = centre(wide_second)
    second_image = centre(operator(wide_second))

    for k, field in enumerate((forcing, image, second, second_image, first)):
        fields[k] = field
    slot_copies = [
        remote(SLOT, fields, fields_near.at[0], beside(0, 1)),
        remote(SLOT + 1, fields, fields_near.at[1], beside(0, -1)),
    ]

    def rows_sum(v):
        return jnp.sum(v, axis=0, keepdims=True)

    products = (
        rows_sum(forcing * first),
        rows_sum(first * image),
        rows_sum(image * second),
        rows_sum(second * second_image),
    )
    tile_row = lax.broadcasted_iota(jnp.int32, (8, cols), 0)
    sums = jnp.zeros((8, cols), jnp.float32)
    for k, product in enumerate(products):
        sums = jnp.where(tile_row == k, product, sums)
    reduce_copies = []
    for stage in range(3):
        partial[stage] = sums
        copies = [
            remote(
                REDUCE + stage * (GROUP - 1) + k - 1,
                partial.at[stage],
                gathered.at[stage, k - 1],
                partner(stage, k),
            )
            for k in range(1, GROUP)
        ]
        reduce_copies += copies
        for k, copy in enumerate(copies):
            copy.wait_recv()
            sums = sums + gathered[stage, k]
    totals = jnp.sum(sums, axis=1, keepdims=True)
    rho, bend, gap, tail = (totals[k : k + 1] for k in range(4))
    step0 = rho / bend
    rho_next = rho - 2.0 * step0 * bend + step0 * step0 * gap
    ratio = rho_next / rho
    cross = bend - step0 * gap
    inner = bend - 2.0 * step0 * gap + step0 * step0 * tail
    step1 = rho_next / (inner + 2.0 * ratio * cross + ratio * ratio * bend)
    along_first = step0 + step1 * (1.0 + ratio)
    along_second = -step1 * step0

    for copy in slot_copies:
        copy.wait_recv()
    for k, ref in enumerate((fields_near.at[0], fields, fields_near.at[1])):
        placed[0, k * rows : (k + 1) * rows, :] = along_first * ref[4] + along_second * ref[2]
        placed[1, k * rows : (k + 1) * rows, :] = (
            ref[0] - along_first * ref[1] - along_second * ref[3]
        )
    blocks = rows // block_rows
    slots = sea_ref.shape[1]
    for slot in range(slots):
        held = map_ref[0, gx * slots + slot]
        filled = jnp.where(held >= 0, 1.0, 0.0)
        safe = jnp.maximum(held, 0)
        offset = lax.rem(safe // blocks - gx + 1 + n_gx, n_gx)
        target = jnp.minimum(offset * blocks + lax.rem(safe, blocks), 3 * blocks - 1)
        begin = pl.ds(target * block_rows, block_rows)
        sea_ref[0, slot] = filled * placed[0, begin, :]
        slot_ref[0, slot] = filled * placed[1, begin, :]

    for copy in (
        meta_copies + atm_copies + edge_copies + search_copies + slot_copies + reduce_copies
    ):
        copy.wait_send()
    store.wait()


def on_device(
    atm_flux,
    remap_source,
    remap_weight,
    tracers,
    velocity,
    vert_diff,
    ocean_depth,
    surface_term,
    land_mask,
    barotropic_block_map,
):
    n_gy, n_gx = lax.axis_size("gy"), lax.axis_size("gx")
    tracer_count, levels, rows, cols = tracers.shape
    blocks = land_mask.shape[0]
    slots = barotropic_block_map.shape[1] // n_gx
    atm_blocks = atm_flux.shape[1]
    f32 = jnp.float32
    vmem = functools.partial(pltpu.VMEM, dtype=f32)
    in_vmem = pl.BlockSpec(memory_space=pltpu.VMEM)
    in_smem = pl.BlockSpec(memory_space=pltpu.SMEM)
    in_hbm = pl.BlockSpec(memory_space=pltpu.HBM)
    slot_shape = jax.ShapeDtypeStruct((1, slots, rows // blocks, cols), f32)
    return pl.pallas_call(
        functools.partial(kernel, n_gy, n_gx),
        out_shape=(jax.ShapeDtypeStruct(tracers.shape, f32), slot_shape, slot_shape),
        in_specs=[in_smem] * 3 + [in_vmem] * 3 + [in_hbm] * 4,
        out_specs=(in_hbm, in_vmem, in_vmem),
        scratch_shapes=[
            pltpu.VMEM(remap_weight.shape, remap_weight.dtype),
            vmem((tracer_count, levels, rows + 16, cols)),
            vmem((levels, rows, cols)),
            vmem((levels, rows + 8, cols)),
            vmem((levels + 1, rows, cols)),
            vmem((3, rows, cols)),
            vmem((3, rows + 16, 3 * cols)),
            vmem((atm_blocks, tracer_count, cols)),
            vmem((3 * atm_blocks, tracer_count, cols)),
            vmem((tracer_count, levels, 2, cols)),
            vmem((tracer_count, levels, 2, cols)),
            vmem((tracer_count, levels, 2, cols)),
            vmem((tracer_count, levels, 2, cols)),
            vmem((64, cols)),
            vmem((64, cols)),
            vmem((2, tracer_count, rows, cols)),
            vmem((2, tracer_count, rows, cols)),
            vmem((rows, cols)),
            vmem((rows, cols)),
            vmem((tracer_count, rows, cols)),
            vmem((tracer_count, rows, cols)),
            vmem((levels, rows, cols)),
            vmem(tracers.shape),
            vmem((rows, cols)),
            vmem((rows + 16, 3 * cols)),
            vmem((5, rows, cols)),
            vmem((2, 5, rows, cols)),
            vmem((3, 8, cols)),
            vmem((3, GROUP - 1, 8, cols)),
            vmem((2, 3 * rows, cols)),
            pltpu.SemaphoreType.DMA((6,)),
            pltpu.SemaphoreType.DMA((COPIES,)),
            pltpu.SemaphoreType.DMA((COPIES,)),
        ],
        compiler_params=pltpu.CompilerParams(
            collective_id=0, has_side_effects=True, vmem_limit_bytes=48 * 1024 * 1024
        ),
        name="ocean_window",
    )(
        remap_source,
        land_mask,
        barotropic_block_map,
        atm_flux,
        ocean_depth,
        surface_term,
        remap_weight,
        tracers,
        velocity,
        vert_diff,
    )


def solution(mesh):
    return jax.shard_map(
        on_device,
        mesh=mesh,
        in_specs=(
            P("gy", "gx", None, None),
            P("gy", "gx", None),
            P("gy", "gx", None, None, None),
            P(None, None, "gy", "gx"),
            P(None, None, "gy", "gx"),
            P(None, "gy", "gx"),
            P("gy", "gx"),
            P("gy", "gx"),
            P("gy", "gx"),
            P("gy", None),
        ),
        out_specs=(P(None, None, "gy", "gx"), P("gy", "gx", None, None), P("gy", "gx", None, None)),
        check_vma=False,
    )
```

time: 493 us -> 60.8 us (0.12)
  blocking collectives: 297 us -> 0 us
  other arithmetic: 95.6 us -> 0 us
  starting transfers between devices: 50.9 us -> 0 us
  Pallas kernels: 0 us -> 49.9 us
  local copies, waits for them, and re-layouts: 25.6 us -> 9.06 us
  waiting for transfers between devices: 11.2 us -> 0 us
  between operations: 6.72 us -> 0.67 us
    psum x3 -> x0, blocking collectives: 297 us -> none  [total_one(): return lax.psum(device_local_value, ('gy', 'gx'))]
    ppermute x16 -> x0, starting transfers between devices: 50.9 us -> none  [the longest x8 29.1 us: extended(): lax.ppermute(head, axis, [((i + 1) % count, i) for i in range(count)])]
    pallas_call x0 -> x1, Pallas kernels: none -> 49.9 us  [on_device(): pl.pallas_call(functools.partial(kernel, n_gy, n_gx), out_shape=(jax.Shap...]
    mul x33 -> x0, other arithmetic: 47.6 us -> none  [the longest x23 23 us: implicit_mix(): result.append(dprime[level_index] - cprime[level_index] * result[-1])]
    add x20 -> x0, other arithmetic: 22 us -> none  [the longest x18 21.9 us: implicit_mix(): divisor = centre + lower_coef * cprime[-1]]
    slice x11 -> x0, local copies, waits for them, and re-layouts: 14.9 us -> none  [the longest x6 6.61 us: extended(): lax.slice_in_dim(cells, cells.shape[dim] - width, cells.shape[dim], axis=...]
    select_n x4 -> x0, other arithmetic: 11.7 us -> none  [the longest x3 11.7 us: close_poles(): return jnp.where(inside, padded, 0.0)]
    ppermute x16 -> x0, waiting for transfers between devices: 11.2 us -> none  [the longest x8 7.4 us: extended(): lax.ppermute(tail, axis, [(i, (i + 1) % count) for i in range(count)])]
  transfers between devices with their start and end apart: 16 -> 0, of which waited for: 8 -> 0; matrix products, arithmetic and copies ran while one was open for 14% -> 0% of each run, Pallas kernels for 0% -> 0%
where the time goes in v1:
time: 60.8 us; the launch traced here: 59.6 us
  Pallas kernels  49.9 us (82%)
  local copies, waits for them, and re-layouts  9.06 us (15%)
  between operations  0.67 us (1%)
    pallas_call x1, Pallas kernels, on_device(): pl.pallas_call(functools.partial(kernel, n_gy, n_gx), out_shape=(jax.Shap...  49.9 us
    unnamed x21, local copies, waits for them, and re-layouts  9.06 us

profile of v1, /device:TPU:1, one launch (start us, length us, event | category | flops | bytes accessed | tf_op | source)
XLA Modules:
  0.0 59.6 jit_solution(2799425898581162571)
XLA Ops:
  0.6 0.0 copy-start.4
  0.6 0.7 %copy.14.land_ref = s32[4,1]{1,0:T(4,128)S(1)} copy(s32[4,1]{0,1:T(1,128)} %param.18) | data formatting | bytes 32 | tf_op args[8]
  1.4 0.0 copy-start.6
  1.4 0.0 copy-start.7
  1.4 0.8 %copy.13.source_ref = s32[16,1,2]{2,1,0:T(1,128)S(1)} copy(s32[16,1,2]{0,2,1:T(2,128)} %param.11) | data formatting | bytes 256 | tf_op args[1]
  2.2 0.0 copy-done.4
  2.2 0.0 copy-done.6
  2.2 0.0 copy-done.7
  2.2 0.0 copy-start
  2.2 1.2 %copy-done = bf16[16,1,2,128,128]{4,3,2,1,0:T(8,128)(2,1)S(1)} copy-done((bf16[16,1,2,128,128]{4,3,2,1,0:T(8,128)(2,1)S(1)}, bf16[16,1,2,128,128]{4,3,2,1,0:T(8,128)(2,1)}, u32[]{:S(2)}) %copy-start) | copy-done | bytes 1048600
  3.4 0.0 copy-start.1
  3.4 1.2 %copy-done.1 = f32[2,62,16,128]{3,2,1,0:T(8,128)S(1)} copy-done((f32[2,62,16,128]{3,2,1,0:T(8,128)S(1)}, f32[2,62,16,128]{3,2,1,0:T(8,128)}, u32[]{:S(2)}) %copy-start.1) | copy-done | bytes 1015832
  4.6 0.0 copy-start.2
  4.6 1.2 %copy-done.2 = f32[2,62,16,128]{3,2,1,0:T(8,128)S(1)} copy-done((f32[2,62,16,128]{3,2,1,0:T(8,128)S(1)}, f32[2,62,16,128]{3,2,1,0:T(8,128)}, u32[]{:S(2)}) %copy-start.2) | copy-done | bytes 1015832
  5.8 0.0 copy-start.3
  5.8 1.0 %copy-done.3 = f32[61,16,128]{2,1,0:T(8,128)S(1)} copy-done((f32[61,16,128]{2,1,0:T(8,128)S(1)}, f32[61,16,128]{2,1,0:T(8,128)}, u32[]{:S(2)}) %copy-start.3) | copy-done | bytes 499736
  6.9 0.0 copy-start.5
  6.9 0.7 %copy-done.5 = f32[16,128]{1,0:T(8,128)S(1)} copy-done((f32[16,128]{1,0:T(8,128)S(1)}, f32[16,128]{1,0:T(8,128)}, u32[]{:S(2)}) %copy-start.5) | copy-done | bytes 8216
  7.6 49.9 %ocean_window.1 = (f32[2,62,16,128]{3,2,1,0:T(8,128)S(1)}, f32[1,3,4,128]{3,2,1,0:T(4,128)S(1)}, f32[1,3,4,128]{3,2,1,0:T(4,128)S(1)}) custom-call(s32[16,1,2]{2,1,0:T(1,128)S(1)} %copy.13.source_ref, s32[4,1]{1,0:T(4,128)S(1)} %copy.14.land_ref, s32[1,96]{1,0:T(1,128)S(1)} %copy-done.7, bf16[1,2,2,128]{3,2,1,0:T(2,128)(2,1)S(1)} %copy-done.6, ...), custom_call_target="tpu_custom_call" | custom-call | tf_op jit(solution)/shard_map/ocean_window/pallas_call | solution.py:534
  57.5 1.0 %copy.18 = f32[2,62,16,128]{3,2,1,0:T(8,128)} copy(f32[2,62,16,128]{3,2,1,0:T(8,128)S(1)} %get-tuple-element.6) | data formatting | bytes 2031616
  58.4 0.6 copy.19
  59.0 0.6 copy.20
Async XLA Ops:
  0.6 1.5 %copy-start.4 = (f32[16,128]{1,0:T(8,128)S(1)}, f32[16,128]{1,0:T(8,128)}, u32[]{:S(2)}) copy-start(f32[16,128]{1,0:T(8,128)} %depth_ref.1) | copy-start | bytes 24580
  1.4 0.8 %copy-start.6 = (bf16[1,2,2,128]{3,2,1,0:T(2,128)(2,1)S(1)}, bf16[1,2,2,128]{3,2,1,0:T(2,128)(2,1)}, u32[]{:S(2)}) copy-start(bf16[1,2,2,128]{3,2,1,0:T(2,128)(2,1)} %atm_ref.1) | copy-start | bytes 3076
  1.4 0.8 %copy-start.7 = (s32[1,96]{1,0:T(1,128)S(1)}, s32[1,96]{1,0:T(1,128)}, u32[]{:S(2)}) copy-start(s32[1,96]{1,0:T(1,128)} %map_ref.1) | copy-start | bytes 1156
  2.2 1.2 %copy-start = (bf16[16,1,2,128,128]{4,3,2,1,0:T(8,128)(2,1)S(1)}, bf16[16,1,2,128,128]{4,3,2,1,0:T(8,128)(2,1)}, u32[]{:S(2)}) copy-start(bf16[16,1,2,128,128]{4,3,2,1,0:T(8,128)(2,1)} %weight_hbm.1) | copy-start | bytes 3145732
  3.4 1.2 %copy-start.1 = (f32[2,62,16,128]{3,2,1,0:T(8,128)S(1)}, f32[2,62,16,128]{3,2,1,0:T(8,128)}, u32[]{:S(2)}) copy-start(f32[2,62,16,128]{3,2,1,0:T(8,128)} %tracer_hbm.1) | copy-start | bytes 3047428
  4.6 1.2 %copy-start.2 = (f32[2,62,16,128]{3,2,1,0:T(8,128)S(1)}, f32[2,62,16,128]{3,2,1,0:T(8,128)}, u32[]{:S(2)}) copy-start(f32[2,62,16,128]{3,2,1,0:T(8,128)} %velocity_hbm.1) | copy-start | bytes 3047428
  5.8 1.0 %copy-start.3 = (f32[61,16,128]{2,1,0:T(8,128)S(1)}, f32[61,16,128]{2,1,0:T(8,128)}, u32[]{:S(2)}) copy-start(f32[61,16,128]{2,1,0:T(8,128)} %vert_hbm.1) | copy-start | bytes 1499140
  6.9 0.7 %copy-start.5 = (f32[16,128]{1,0:T(8,128)S(1)}, f32[16,128]{1,0:T(8,128)}, u32[]{:S(2)}) copy-start(f32[16,128]{1,0:T(8,128)} %surface_ref.1) | copy-start | bytes 24580

commit v2 on v1

--- a/solution.py
+++ b/solution.py
@@ -12,8 +12,9 @@
 FLUX_GAIN = 0.5
 MESH = pl.DeviceIdType.MESH
 GROUP = 8
+VMEM_LIMIT = 67043328
 SIDES = ((0, 1), (0, -1), (1, 0), (-1, 0), (1, 1), (1, -1), (-1, 1), (-1, -1))
-META, ATM, EDGE, SEARCH, SLOT, REDUCE = 0, 8, 10, 16, 24, 26
+META, ATM, EDGE, SEARCH, SLOT, REDUCE = 0, 8, 10, 18, 26, 28
 COPIES = REDUCE + 3 * (GROUP - 1)
 
 
@@ -40,8 +41,7 @@
     velocity_hbm,
     vert_hbm,
     new_hbm,
-    sea_ref,
-    slot_ref,
+    slots_ref,
     weight,
     cells,
     east_speed,
@@ -64,6 +64,8 @@
     west_face,
     surface_flux,
     factor,
+    scale,
+    gain,
     solved,
     search_own,
     search,
@@ -80,14 +82,22 @@
     gy = lax.axis_index("gy")
     gx = lax.axis_index("gx")
 
+    half = levels // 2
     loads = [
-        pltpu.make_async_copy(tracer_hbm, cells.at[:, :, 8 : 8 + rows, :], local_sem.at[0]),
-        pltpu.make_async_copy(velocity_hbm.at[0], east_speed, local_sem.at[1]),
         pltpu.make_async_copy(
-            velocity_hbm.at[1], north_speed.at[:, 8 : 8 + rows, :], local_sem.at[2]
+            tracer_hbm.at[:, part * half : (part + 1) * half],
+            cells.at[:, part * half : (part + 1) * half, 8 : 8 + rows, :],
+            local_sem.at[part],
+        )
+        for part in range(2)
+    ]
+    loads += [
+        pltpu.make_async_copy(velocity_hbm.at[0], east_speed, local_sem.at[2]),
+        pltpu.make_async_copy(
+            velocity_hbm.at[1], north_speed.at[:, 8 : 8 + rows, :], local_sem.at[3]
         ),
-        pltpu.make_async_copy(weight_hbm, weight, local_sem.at[3]),
         pltpu.make_async_copy(vert_hbm, vert.at[1:levels], local_sem.at[4]),
+        pltpu.make_async_copy(weight_hbm, weight, local_sem.at[5]),
     ]
     for load in loads:
         load.start()
@@ -146,10 +156,10 @@
 
     row = lax.broadcasted_iota(jnp.int32, (rows, cols), 0)
     lane = lax.broadcasted_iota(jnp.int32, (rows, cols), 1)
-    block_rows = rows // land_ref.shape[0]
+    block_rows = rows // land_ref.shape[1]
     mask = jnp.zeros((rows, cols), jnp.float32)
-    for block in range(land_ref.shape[0]):
-        wet = land_ref[block, 0].astype(jnp.float32)
+    for block in range(land_ref.shape[1]):
+        wet = land_ref[0, block].astype(jnp.float32)
         mask = jnp.where(row // block_rows == block, wet, mask)
     meta_own[0] = mask
     meta_own[1] = depth_ref[...]
@@ -160,15 +170,6 @@
     blocks_near = atm_own.shape[0]
     atm_near[blocks_near : 2 * blocks_near] = atm_own[...]
 
-    pl.semaphore_wait(barrier, len(peers))
-    sent = sides(META, meta_own, meta)
-    meta_copies = list(sent)
-    atm_copies = [
-        remote(ATM, atm_own, atm_near.at[0:blocks_near], beside(0, 1)),
-        remote(ATM + 1, atm_own, atm_near.at[2 * blocks_near : 3 * blocks_near], beside(0, -1)),
-    ]
-
-    loads[0].wait()
     zero = jnp.zeros((rows, cols), jnp.float32)
     pair = lane // 2
 
@@ -178,27 +179,43 @@
         for f in range(tracer_count):
             values = cells[f, level, 8 : 8 + rows, :] * mask
             cells[f, level, 8 : 8 + rows, :] = values
-            to_north[f, level] = values[rows - 2 :]
-            to_south[f, level] = values[:2]
+            to_north[level, f] = values[rows - 2 :]
+            to_south[level, f] = values[:2]
             packed[2 * f] = jnp.where(here, pltpu.roll(values, 2 * level, 1), packed[2 * f])
             packed[2 * f + 1] = jnp.where(
                 here, pltpu.roll(values, lax.rem(2 * level + 2, cols), 1), packed[2 * f + 1]
             )
         return tuple(packed)
 
-    packed = lax.fori_loop(0, levels, pack, (zero,) * (2 * tracer_count), unroll=2)
+    def row_copies(part):
+        span = slice(part * half, (part + 1) * half)
+        return [
+            remote(EDGE + 2 * part, to_north.at[span], from_south.at[span], beside(1, 0)),
+            remote(EDGE + 2 * part + 1, to_south.at[span], from_north.at[span], beside(-1, 0)),
+        ]
+
+    loads[0].wait()
+    packed = lax.fori_loop(0, half, pack, (zero,) * (2 * tracer_count), unroll=4)
+    pl.semaphore_wait(barrier, len(peers))
+    near_copies = [row_copies(0)]
+    meta_copies = sides(META, meta_own, meta)
+    atm_copies = [
+        remote(ATM, atm_own, atm_near.at[0:blocks_near], beside(0, 1)),
+        remote(ATM + 1, atm_own, atm_near.at[2 * blocks_near : 3 * blocks_near], beside(0, -1)),
+    ]
+    loads[1].wait()
+    packed = lax.fori_loop(half, levels, pack, packed, unroll=4)
+    near_copies.append(row_copies(1))
     for f in range(tracer_count):
         edge_own[0, f] = packed[2 * f]
         edge_own[1, f] = packed[2 * f + 1]
     edge_copies = [
-        remote(EDGE, to_north, from_south, beside(1, 0)),
-        remote(EDGE + 1, to_south, from_north, beside(-1, 0)),
-        remote(EDGE + 2, edge_own.at[0], edge_near.at[0], beside(0, -1)),
-        remote(EDGE + 3, edge_own.at[1], edge_near.at[1], beside(0, 1)),
+        remote(EDGE + 4, edge_own.at[0], edge_near.at[0], beside(0, -1)),
+        remote(EDGE + 5, edge_own.at[1], edge_near.at[1], beside(0, 1)),
     ]
 
-    loads[1].wait()
     loads[2].wait()
+    loads[3].wait()
 
     def pack_speed(level, packed):
         speed_north[pl.ds(level, 1), :] = north_speed[level, 7 + rows : 8 + rows, :]
@@ -210,18 +227,41 @@
 
     speed_east[...] = lax.fori_loop(0, levels, pack_speed, zero, unroll=2)
     edge_copies += [
-        remote(EDGE + 4, speed_north, speed_south, beside(1, 0)),
-        remote(EDGE + 5, speed_east, speed_west, beside(0, 1)),
+        remote(EDGE + 6, speed_north, speed_south, beside(1, 0)),
+        remote(EDGE + 7, speed_east, speed_west, beside(0, 1)),
     ]
 
-    loads[3].wait()
+    loads[4].wait()
+    vert[0] = zero
+    vert[levels] = zero
+
+    def eliminate(step, carry):
+        top, bottom = carry
+        low, high = step, levels - 1 - step
+        lower, upper = vert[low], vert[low + 1]
+        share = 1.0 / (1.0 + lower + upper + lower * top)
+        top = -upper * share
+        factor[low] = top
+        scale[low] = share
+        gain[low] = lower * share
+        lower, upper = vert[high], vert[high + 1]
+        share = 1.0 / (1.0 + lower + upper + upper * bottom)
+        bottom = -lower * share
+        factor[high] = bottom
+        scale[high] = share
+        gain[high] = upper * share
+        return top, bottom
+
+    top, bottom = lax.fori_loop(0, half, eliminate, (zero, zero))
+
+    loads[5].wait()
     for copy in atm_copies:
         copy.wait_recv()
 
     def remap(r, carry):
         total = jnp.zeros((tracer_count, cols), jnp.float32)
         for k in range(weight.shape[2]):
-            picked = atm_near[source_ref[r, 0, k]].astype(jnp.bfloat16)
+            picked = atm_near[source_ref[0, k, r]].astype(jnp.bfloat16)
             total += lax.dot_general(
                 picked,
                 weight[r, 0, k],
@@ -289,14 +329,6 @@
     for copy in edge_copies:
         copy.wait_recv()
 
-    def place(level, carry):
-        for f in range(tracer_count):
-            cells[f, level, 6:8, :] = from_south[f, level] * mask_south
-            cells[f, level, 8 + rows : 10 + rows, :] = from_north[f, level] * mask_north
-        north_speed[level, 7:8, :] = speed_south[pl.ds(level, 1), :]
-        return carry
-
-    lax.fori_loop(0, levels, place, 0, unroll=2)
     for f in range(tracer_count):
         behind = edge_near[1, f]
         ahead = edge_own[0, f]
@@ -308,10 +340,6 @@
             pltpu.roll(ahead, cols - 1, 1),
             (12.0 * DIFFUSIVITY) * west_open,
         )
-
-    loads[4].wait()
-    vert[0] = zero
-    vert[levels] = zero
 
     def advected(level):
         along = east_speed[level] * east_open
@@ -352,39 +380,45 @@
     mix_north = (12.0 * DIFFUSIVITY) * north_open
     mix_south = (12.0 * DIFFUSIVITY) * south_open
 
-    half = levels // 2
-
-    def eliminate(step, carry):
-        top, top_values, bottom, bottom_values = carry
+    def advect(level, total):
+        for f in range(tracer_count):
+            cells[f, level, 6:8, :] = from_south[level, f] * mask_south
+            cells[f, level, 8 + rows : 10 + rows, :] = from_north[level, f] * mask_north
+        north_speed[level, 7:8, :] = speed_south[pl.ds(level, 1), :]
+        provisional = advected(level)
+        for f in range(tracer_count):
+            solved[f, level] = provisional[f]
+        return total + (provisional[0] - provisional[1])
+
+    total = surface_flux[0] - surface_flux[1]
+    for part in range(2):
+        for copy in near_copies[part]:
+            copy.wait_recv()
+        total = lax.fori_loop(part * half, (part + 1) * half, advect, total)
+    for f in range(tracer_count):
+        solved[f, 0] = solved[f, 0] + surface_flux[f]
+
+    forcing = mask * total * (1.0 / math.sqrt(2.0 * levels))
+    first = centre(inverse) * forcing
+    search_own[...] = first
+    search[8 : 8 + rows, cols : 2 * cols] = first
+    search_copies = sides(SEARCH, search_own, search)
+
+    def inward(step, carry):
         low, high = step, levels - 1 - step
-        share = jnp.where(step == 0, 1.0, 0.0)
-        lower, upper = vert[low], vert[low + 1]
-        scale = 1.0 / (1.0 + lower + upper + lower * top)
-        top = -upper * scale
-        factor[low] = top
-        provisional = advected(low)
-        top_values = tuple(
-            (provisional[f] + share * surface_flux[f] + lower * top_values[f]) * scale
-            for f in range(tracer_count)
-        )
-        for f in range(tracer_count):
-            solved[f, low] = top_values[f]
-        lower, upper = vert[high], vert[high + 1]
-        scale = 1.0 / (1.0 + lower + upper + upper * bottom)
-        bottom = -lower * scale
-        factor[high] = bottom
-        provisional = advected(high)
-        bottom_values = tuple(
-            (provisional[f] + upper * bottom_values[f]) * scale for f in range(tracer_count)
-        )
-        for f in range(tracer_count):
-            solved[f, high] = bottom_values[f]
-        return top, top_values, bottom, bottom_values
+        values = []
+        for level, before in ((low, carry[0]), (high, carry[1])):
+            value = tuple(
+                solved[f, level] * scale[level] + gain[level] * before[f]
+                for f in range(tracer_count)
+            )
+            for f in range(tracer_count):
+                solved[f, level] = value[f]
+            values.append(value)
+        return tuple(values)
 
     none = (zero,) * tracer_count
-    top, top_values, bottom, bottom_values = lax.fori_loop(
-        0, half, eliminate, (zero, none, zero, none)
-    )
+    top_values, bottom_values = lax.fori_loop(0, half, inward, (none, none), unroll=2)
     across = 1.0 / (1.0 - top * bottom)
     up, down = [], []
     for f in range(tracer_count):
@@ -394,29 +428,22 @@
         solved[f, half] = lower_value
         up.append(upper_value)
         down.append(lower_value)
-    total = (up[0] - up[1]) + (down[0] - down[1])
-
-    def substitute(step, carry):
-        up, down, total = carry
-        low, high = half - 2 - step, half + 1 + step
-        up = tuple(solved[f, low] - factor[low] * up[f] for f in range(tracer_count))
-        down = tuple(solved[f, high] - factor[high] * down[f] for f in range(tracer_count))
-        for f in range(tracer_count):
-            solved[f, low] = up[f]
-            solved[f, high] = down[f]
-        return up, down, total + ((up[0] - up[1]) + (down[0] - down[1]))
-
-    _, _, total = lax.fori_loop(
-        0, half - 1, substitute, (tuple(up), tuple(down), total), unroll=2
-    )
-    store = pltpu.make_async_copy(solved, new_hbm, local_sem.at[5])
+
+    def outward(step, carry):
+        values = []
+        for level, before in ((half - 2 - step, carry[0]), (half + 1 + step, carry[1])):
+            value = tuple(
+                solved[f, level] - factor[level] * before[f] for f in range(tracer_count)
+            )
+            for f in range(tracer_count):
+                solved[f, level] = value[f]
+            values.append(value)
+        return tuple(values)
+
+    lax.fori_loop(0, half - 1, outward, (tuple(up), tuple(down)), unroll=2)
+    store = pltpu.make_async_copy(solved, new_hbm, local_sem.at[6])
     store.start()
 
-    forcing = mask * total * (1.0 / math.sqrt(2.0 * levels))
-    first = centre(inverse) * forcing
-    search_own[...] = first
-    search[8 : 8 + rows, cols : 2 * cols] = first
-    search_copies = sides(SEARCH, search_own, search)
     for copy in search_copies:
         copy.wait_recv()
 
@@ -435,12 +462,8 @@
     second = centre(wide_second)
     second_image = centre(operator(wide_second))
 
-    for k, field in enumerate((forcing, image, second, second_image, first)):
+    for k, field in enumerate((forcing, image, second, second_image)):
         fields[k] = field
-    slot_copies = [
-        remote(SLOT, fields, fields_near.at[0], beside(0, 1)),
-        remote(SLOT + 1, fields, fields_near.at[1], beside(0, -1)),
-    ]
 
     def rows_sum(v):
         return jnp.sum(v, axis=0, keepdims=True)
@@ -455,9 +478,15 @@
     sums = jnp.zeros((8, cols), jnp.float32)
     for k, product in enumerate(products):
         sums = jnp.where(tile_row == k, product, sums)
+    sums = jnp.sum(sums, axis=1, keepdims=True)
+    place = lax.broadcasted_iota(jnp.int32, (1, cols), 1)
+    line = jnp.zeros((1, cols), jnp.float32)
+    for k in range(4):
+        line = jnp.where(place == k, sums[k : k + 1], line)
     reduce_copies = []
+    slot_copies = []
     for stage in range(3):
-        partial[stage] = sums
+        partial[stage] = line
         copies = [
             remote(
                 REDUCE + stage * (GROUP - 1) + k - 1,
@@ -468,11 +497,17 @@
             for k in range(1, GROUP)
         ]
         reduce_copies += copies
+        if stage == 0:
+            slot_copies = [
+                remote(SLOT, fields, fields_near.at[0], beside(0, 1)),
+                remote(SLOT + 1, fields, fields_near.at[1], beside(0, -1)),
+            ]
         for k, copy in enumerate(copies):
             copy.wait_recv()
-            sums = sums + gathered[stage, k]
-    totals = jnp.sum(sums, axis=1, keepdims=True)
-    rho, bend, gap, tail = (totals[k : k + 1] for k in range(4))
+            line = line + gathered[stage, k]
+    rho, bend, gap, tail = (
+        jnp.sum(jnp.where(place == k, line, 0.0), axis=1, keepdims=True) for k in range(4)
+    )
     step0 = rho / bend
     rho_next = rho - 2.0 * step0 * bend + step0 * step0 * gap
     ratio = rho_next / rho
@@ -485,12 +520,13 @@
     for copy in slot_copies:
         copy.wait_recv()
     for k, ref in enumerate((fields_near.at[0], fields, fields_near.at[1])):
-        placed[0, k * rows : (k + 1) * rows, :] = along_first * ref[4] + along_second * ref[2]
+        nearby = search[8 : 8 + rows, k * cols : (k + 1) * cols]
+        placed[0, k * rows : (k + 1) * rows, :] = along_first * nearby + along_second * ref[2]
         placed[1, k * rows : (k + 1) * rows, :] = (
             ref[0] - along_first * ref[1] - along_second * ref[3]
         )
     blocks = rows // block_rows
-    slots = sea_ref.shape[1]
+    slots = slots_ref.shape[1]
     for slot in range(slots):
         held = map_ref[0, gx * slots + slot]
         filled = jnp.where(held >= 0, 1.0, 0.0)
@@ -498,11 +534,16 @@
         offset = lax.rem(safe // blocks - gx + 1 + n_gx, n_gx)
         target = jnp.minimum(offset * blocks + lax.rem(safe, blocks), 3 * blocks - 1)
         begin = pl.ds(target * block_rows, block_rows)
-        sea_ref[0, slot] = filled * placed[0, begin, :]
-        slot_ref[0, slot] = filled * placed[1, begin, :]
+        slots_ref[0, slot] = filled * placed[0, begin, :]
+        slots_ref[1, slot] = filled * placed[1, begin, :]
 
     for copy in (
-        meta_copies + atm_copies + edge_copies + search_copies + slot_copies + reduce_copies
+        meta_copies
+        + atm_copies
+        + near_copies[0]
+        + near_copies[1]
+        + edge_copies
+        + search_copies + slot_copies + reduce_copies
     ):
         copy.wait_send()
     store.wait()
@@ -530,12 +571,12 @@
     in_vmem = pl.BlockSpec(memory_space=pltpu.VMEM)
     in_smem = pl.BlockSpec(memory_space=pltpu.SMEM)
     in_hbm = pl.BlockSpec(memory_space=pltpu.HBM)
-    slot_shape = jax.ShapeDtypeStruct((1, slots, rows // blocks, cols), f32)
-    return pl.pallas_call(
+    slot_shape = jax.ShapeDtypeStruct((2, slots, rows // blocks, cols), f32)
+    new_tracers, in_slots = pl.pallas_call(
         functools.partial(kernel, n_gy, n_gx),
-        out_shape=(jax.ShapeDtypeStruct(tracers.shape, f32), slot_shape, slot_shape),
+        out_shape=(jax.ShapeDtypeStruct(tracers.shape, f32), slot_shape),
         in_specs=[in_smem] * 3 + [in_vmem] * 3 + [in_hbm] * 4,
-        out_specs=(in_hbm, in_vmem, in_vmem),
+        out_specs=(in_hbm, in_vmem),
         scratch_shapes=[
             pltpu.VMEM(remap_weight.shape, remap_weight.dtype),
             vmem((tracer_count, levels, rows + 16, cols)),
@@ -546,10 +587,10 @@
             vmem((3, rows + 16, 3 * cols)),
             vmem((atm_blocks, tracer_count, cols)),
             vmem((3 * atm_blocks, tracer_count, cols)),
-            vmem((tracer_count, levels, 2, cols)),
-            vmem((tracer_count, levels, 2, cols)),
-            vmem((tracer_count, levels, 2, cols)),
-            vmem((tracer_count, levels, 2, cols)),
+            vmem((levels, tracer_count, 2, cols)),
+            vmem((levels, tracer_count, 2, cols)),
+            vmem((levels, tracer_count, 2, cols)),
+            vmem((levels, tracer_count, 2, cols)),
             vmem((64, cols)),
             vmem((64, cols)),
             vmem((2, tracer_count, rows, cols)),
@@ -559,25 +600,27 @@
             vmem((tracer_count, rows, cols)),
             vmem((tracer_count, rows, cols)),
             vmem((levels, rows, cols)),
+            vmem((levels, rows, cols)),
+            vmem((levels, rows, cols)),
             vmem(tracers.shape),
             vmem((rows, cols)),
             vmem((rows + 16, 3 * cols)),
-            vmem((5, rows, cols)),
-            vmem((2, 5, rows, cols)),
-            vmem((3, 8, cols)),
-            vmem((3, GROUP - 1, 8, cols)),
+            vmem((4, rows, cols)),
+            vmem((2, 4, rows, cols)),
+            vmem((3, 1, cols)),
+            vmem((3, GROUP - 1, 1, cols)),
             vmem((2, 3 * rows, cols)),
-            pltpu.SemaphoreType.DMA((6,)),
+            pltpu.SemaphoreType.DMA((7,)),
             pltpu.SemaphoreType.DMA((COPIES,)),
             pltpu.SemaphoreType.DMA((COPIES,)),
         ],
         compiler_params=pltpu.CompilerParams(
-            collective_id=0, has_side_effects=True, vmem_limit_bytes=48 * 1024 * 1024
+            collective_id=0, has_side_effects=True, vmem_limit_bytes=VMEM_LIMIT
         ),
         name="ocean_window",
     )(
-        remap_source,
-        land_mask,
+        jnp.transpose(remap_source, (1, 2, 0)),
+        land_mask.T,
         barotropic_block_map,
         atm_flux,
         ocean_depth,
@@ -587,6 +630,7 @@
         velocity,
         vert_diff,
     )
+    return new_tracers, in_slots[:1], in_slots[1:]
 
 
 def solution(mesh):

time: 60.8 us -> 58.3 us (0.959); the launches traced: 59.6 us -> 57.8 us
  local copies, waits for them, and re-layouts: 9.06 us -> 3.54 us
  Pallas kernels: 49.9 us -> 53.6 us
    unnamed x21 -> x1, local copies, waits for them, and re-layouts: 9.06 us -> 2.23 us
    pallas_call x1, Pallas kernels: 49.9 us -> 53.6 us  [on_device(): pl.pallas_call(functools.partial(kernel, n_gy, n_gx), out_shape=(jax.Shap...]
    slice x0 -> x1, local copies, waits for them, and re-layouts: none -> 1.31 us  [on_device(): return (new_tracers, in_slots[:1], in_slots[1:])]
where the time goes in v2:
time: 58.3 us; the launch traced here: 57.8 us
  Pallas kernels  53.6 us (92%)
  local copies, waits for them, and re-layouts  3.54 us (6%)
  between operations  0.64 us (1%)
    pallas_call x1, Pallas kernels, on_device(): pl.pallas_call(functools.partial(kernel, n_gy, n_gx), out_shape=(jax.Shap...  53.6 us
    unnamed x1, local copies, waits for them, and re-layouts  2.23 us
    slice x1, local copies, waits for them, and re-layouts, on_device(): return (new_tracers, in_slots[:1], in_slots[1:])  1.31 us

profile of v2, /device:TPU:1, one launch (start us, length us, event | category | flops | bytes accessed | tf_op | source)
XLA Modules:
  0.0 57.8 jit_solution(8559332045175945808)
XLA Ops:
  0.6 53.6 %ocean_window.1 = (f32[2,62,16,128]{3,2,1,0:T(8,128)}, f32[2,3,4,128]{3,2,1,0:T(4,128)}) custom-call(s32[1,2,16]{2,1,0:T(2,128)} %bitcast.2, s32[1,4]{1,0:T(1,128)} %bitcast.3, s32[1,96]{1,0:T(1,128)} %map_ref.1, bf16[1,2,2,128]{3,2,1,0:T(2,128)(2,1)} %atm_ref.1, f32[16,128]{1,0:T(8,128)} %depth_ref.1, f32[16,128]{1,0:T(8,128)} %surface_ref.1, ...), custom_call_target="tpu_custom_call" | custom-call | tf_op jit(solution)/shard_map/ocean_window/pallas_call | solution.py:575
  54.2 1.3 %fusion = (f32[1,3,4,128]{3,2,1,0:T(4,128)}, f32[1,3,4,128]{3,2,1,0:T(4,128)}) fusion(f32[2,3,4,128]{3,2,1,0:T(4,128)} %get-tuple-element.6), kind=kLoop, calls=%fused_computation | loop fusion | bytes 24576 | tf_op jit(solution)/shard_map/slice | solution.py:633
  55.5 2.2 %copy.14 = f32[2,62,16,128]{3,2,1,0:T(8,128)} copy(f32[2,62,16,128]{3,2,1,0:T(8,128)} %get-tuple-element.12) | data formatting | bytes 2031616

commit v3 on v2

--- a/solution.py
+++ b/solution.py
@@ -33,9 +33,9 @@
     source_ref,
     land_ref,
     map_ref,
-    atm_ref,
-    depth_ref,
-    surface_ref,
+    atm_hbm,
+    depth_hbm,
+    surface_hbm,
     weight_hbm,
     tracer_hbm,
     velocity_hbm,
@@ -49,6 +49,7 @@
     vert,
     meta_own,
     meta,
+    atm_raw,
     atm_own,
     atm_near,
     to_north,
@@ -62,6 +63,7 @@
     speed_east,
     speed_west,
     west_face,
+    beyond,
     surface_flux,
     factor,
     scale,
@@ -99,7 +101,12 @@
         pltpu.make_async_copy(vert_hbm, vert.at[1:levels], local_sem.at[4]),
         pltpu.make_async_copy(weight_hbm, weight, local_sem.at[5]),
     ]
-    for load in loads:
+    small = [
+        pltpu.make_async_copy(depth_hbm, meta_own.at[1], local_sem.at[7]),
+        pltpu.make_async_copy(surface_hbm, meta_own.at[2], local_sem.at[8]),
+        pltpu.make_async_copy(atm_hbm, atm_raw, local_sem.at[9]),
+    ]
+    for load in small + loads:
         load.start()
 
     def beside(dy, dx):
@@ -162,30 +169,28 @@
         wet = land_ref[0, block].astype(jnp.float32)
         mask = jnp.where(row // block_rows == block, wet, mask)
     meta_own[0] = mask
-    meta_own[1] = depth_ref[...]
-    meta_own[2] = surface_ref[...]
+    for load in small:
+        load.wait()
     for k in range(3):
         meta[k, 8 : 8 + rows, cols : 2 * cols] = meta_own[k]
-    atm_own[...] = atm_ref[0].astype(jnp.float32)
+    atm_own[...] = atm_raw[0].astype(jnp.float32)
     blocks_near = atm_own.shape[0]
     atm_near[blocks_near : 2 * blocks_near] = atm_own[...]
 
     zero = jnp.zeros((rows, cols), jnp.float32)
-    pair = lane // 2
-
-    def pack(level, packed):
-        packed = list(packed)
-        here = pair == level
+    group = lane // 4
+
+    def pack(part, level, packed):
+        index = level - part * half
+        kept = []
         for f in range(tracer_count):
             values = cells[f, level, 8 : 8 + rows, :] * mask
             cells[f, level, 8 : 8 + rows, :] = values
             to_north[level, f] = values[rows - 2 :]
             to_south[level, f] = values[:2]
-            packed[2 * f] = jnp.where(here, pltpu.roll(values, 2 * level, 1), packed[2 * f])
-            packed[2 * f + 1] = jnp.where(
-                here, pltpu.roll(values, lax.rem(2 * level + 2, cols), 1), packed[2 * f + 1]
-            )
-        return tuple(packed)
+            turned = pltpu.roll(values, 4 * index + 2, 1)
+            kept.append(jnp.where(group == index, turned, packed[f]))
+        return tuple(kept)
 
     def row_copies(part):
         span = slice(part * half, (part + 1) * half)
@@ -195,7 +200,11 @@
         ]
 
     loads[0].wait()
-    packed = lax.fori_loop(0, half, pack, (zero,) * (2 * tracer_count), unroll=4)
+    packed = lax.fori_loop(
+        0, half, functools.partial(pack, 0), (zero,) * tracer_count, unroll=4
+    )
+    for f in range(tracer_count):
+        edge_own[0, f] = packed[f]
     pl.semaphore_wait(barrier, len(peers))
     near_copies = [row_copies(0)]
     meta_copies = sides(META, meta_own, meta)
@@ -204,28 +213,30 @@
         remote(ATM + 1, atm_own, atm_near.at[2 * blocks_near : 3 * blocks_near], beside(0, -1)),
     ]
     loads[1].wait()
-    packed = lax.fori_loop(half, levels, pack, packed, unroll=4)
+    packed = lax.fori_loop(
+        half, levels, functools.partial(pack, 1), (zero,) * tracer_count, unroll=4
+    )
     near_copies.append(row_copies(1))
     for f in range(tracer_count):
-        edge_own[0, f] = packed[2 * f]
-        edge_own[1, f] = packed[2 * f + 1]
+        edge_own[1, f] = packed[f]
     edge_copies = [
-        remote(EDGE + 4, edge_own.at[0], edge_near.at[0], beside(0, -1)),
-        remote(EDGE + 5, edge_own.at[1], edge_near.at[1], beside(0, 1)),
+        remote(EDGE + 4, edge_own, edge_near.at[0], beside(0, -1)),
+        remote(EDGE + 5, edge_own, edge_near.at[1], beside(0, 1)),
     ]
 
     loads[2].wait()
     loads[3].wait()
 
-    def pack_speed(level, packed):
+    def pack_speed(part, level, packed):
+        index = level - part * half
         speed_north[pl.ds(level, 1), :] = north_speed[level, 7 + rows : 8 + rows, :]
-        return jnp.where(
-            pair == level,
-            pltpu.roll(east_speed[level], lax.rem(2 * level + 1, cols), 1),
-            packed,
-        )
-
-    speed_east[...] = lax.fori_loop(0, levels, pack_speed, zero, unroll=2)
+        turned = pltpu.roll(east_speed[level], 4 * index + 1, 1)
+        return jnp.where(group == index, turned, packed)
+
+    for part in range(2):
+        speed_east[part] = lax.fori_loop(
+            part * half, (part + 1) * half, functools.partial(pack_speed, part), zero, unroll=4
+        )
     edge_copies += [
         remote(EDGE + 6, speed_north, speed_south, beside(1, 0)),
         remote(EDGE + 7, speed_east, speed_west, beside(0, 1)),
@@ -329,23 +340,37 @@
     for copy in edge_copies:
         copy.wait_recv()
 
-    for f in range(tracer_count):
-        behind = edge_near[1, f]
-        ahead = edge_own[0, f]
-        west_face[f] = flux(
-            speed_west[...] * west_open,
-            behind,
-            pltpu.roll(behind, cols - 1, 1),
-            ahead,
-            pltpu.roll(ahead, cols - 1, 1),
-            (12.0 * DIFFUSIVITY) * west_open,
-        )
-
-    def advected(level):
-        along = east_speed[level] * east_open
-        across_north = north_speed[level, 8 : 8 + rows, :] * north_open
-        across_south = north_speed[level, 7 : 7 + rows, :] * south_open
-        twice = 2 * level
+    for part in range(2):
+        for f in range(tracer_count):
+            behind = edge_near[1, part, f]
+            ahead = edge_own[part, f]
+            west_face[part, f] = flux(
+                speed_west[part] * west_open,
+                behind,
+                pltpu.roll(behind, cols - 1, 1),
+                pltpu.roll(ahead, cols - 2, 1),
+                pltpu.roll(ahead, cols - 3, 1),
+                (12.0 * DIFFUSIVITY) * west_open,
+            )
+            beyond[part, f] = jnp.where(lane % 4 < 2, behind, edge_near[0, part, f])
+
+    def coefficients(speed, mixing):
+        size = jnp.abs(speed)
+        common, tilt = 7.0 * speed, 3.0 * size - mixing
+        return size - speed, common - tilt, common + tilt, size + speed
+
+    def advected(part, level):
+        back_e, centre_e, next_e, far_e = coefficients(east_speed[level] * east_open, mix_east)
+        back_n, centre_n, next_n, far_n = coefficients(
+            north_speed[level, 8 : 8 + rows, :] * north_open, mix_north
+        )
+        back_s, centre_s, next_s, far_s = coefficients(
+            north_speed[level, 7 : 7 + rows, :] * south_open, mix_south
+        )
+        at_here = centre_n - next_s
+        at_north = next_n + far_s
+        at_south = back_n - centre_s
+        turn = 4 * (level - part * half)
         results = []
         for f in range(tracer_count):
             here = cells[f, level, 8 : 8 + rows, :]
@@ -353,39 +378,35 @@
             south2 = cells[f, level, 6 : 6 + rows, :]
             north1 = cells[f, level, 9 : 9 + rows, :]
             north2 = cells[f, level, 10 : 10 + rows, :]
-            right = pltpu.roll(edge_near[0, f], lax.rem(2 * cols - 2 - twice, cols), 1)
-            east2 = jnp.where(lane >= cols - 2, right, pltpu.roll(here, cols - 2, 1))
-            east1 = jnp.where(
-                lane == cols - 1, pltpu.roll(right, 1, 1), pltpu.roll(here, cols - 1, 1)
-            )
-            west1 = jnp.where(
-                lane == 0,
-                pltpu.roll(edge_near[1, f], lax.rem(2 * cols - 1 - twice, cols), 1),
-                pltpu.roll(here, 1, 1),
-            )
-            east_flux = flux(along, west1, here, east1, east2, mix_east)
+            outer = pltpu.roll(beyond[part, f], lax.rem(2 * cols - 2 - turn, cols), 1)
+            east2 = pltpu.roll(jnp.where(lane < 2, outer, here), cols - 2, 1)
+            east1 = pltpu.roll(jnp.where(lane < 1, outer, here), cols - 1, 1)
+            west1 = pltpu.roll(jnp.where(lane == cols - 1, outer, here), 1, 1)
+            east_flux = (centre_e * here + next_e * east1) + (back_e * west1 - far_e * east2)
             west_flux = jnp.where(
                 lane == 0,
-                pltpu.roll(west_face[f], lax.rem(2 * cols - twice, cols), 1),
+                pltpu.roll(west_face[part, f], lax.rem(cols - turn, cols), 1),
                 pltpu.roll(east_flux, 1, 1),
             )
-            north_flux = flux(across_north, south1, here, north1, north2, mix_north)
-            south_flux = flux(across_south, south2, south1, here, north1, mix_south)
-            results.append(
-                mask * (here - (east_flux - west_flux) - (north_flux - south_flux))
-            )
+            spread = (at_here * here + at_north * north1) + (
+                at_south * south1 - (far_n * north2 + back_s * south2)
+            )
+            results.append(mask * (here - (east_flux - west_flux) - spread))
         return results
 
     mix_east = (12.0 * DIFFUSIVITY) * east_open
     mix_north = (12.0 * DIFFUSIVITY) * north_open
     mix_south = (12.0 * DIFFUSIVITY) * south_open
 
-    def advect(level, total):
+    def put(level, carry):
         for f in range(tracer_count):
             cells[f, level, 6:8, :] = from_south[level, f] * mask_south
             cells[f, level, 8 + rows : 10 + rows, :] = from_north[level, f] * mask_north
         north_speed[level, 7:8, :] = speed_south[pl.ds(level, 1), :]
-        provisional = advected(level)
+        return carry
+
+    def advect(part, level, total):
+        provisional = advected(part, level)
         for f in range(tracer_count):
             solved[f, level] = provisional[f]
         return total + (provisional[0] - provisional[1])
@@ -394,7 +415,10 @@
     for part in range(2):
         for copy in near_copies[part]:
             copy.wait_recv()
-        total = lax.fori_loop(part * half, (part + 1) * half, advect, total)
+        lax.fori_loop(part * half, (part + 1) * half, put, 0, unroll=4)
+        total = lax.fori_loop(
+            part * half, (part + 1) * half, functools.partial(advect, part), total, unroll=1
+        )
     for f in range(tracer_count):
         solved[f, 0] = solved[f, 0] + surface_flux[f]
 
@@ -575,7 +599,7 @@
     new_tracers, in_slots = pl.pallas_call(
         functools.partial(kernel, n_gy, n_gx),
         out_shape=(jax.ShapeDtypeStruct(tracers.shape, f32), slot_shape),
-        in_specs=[in_smem] * 3 + [in_vmem] * 3 + [in_hbm] * 4,
+        in_specs=[in_smem] * 3 + [in_hbm] * 7,
         out_specs=(in_hbm, in_vmem),
         scratch_shapes=[
             pltpu.VMEM(remap_weight.shape, remap_weight.dtype),
@@ -585,6 +609,7 @@
             vmem((levels + 1, rows, cols)),
             vmem((3, rows, cols)),
             vmem((3, rows + 16, 3 * cols)),
+            pltpu.VMEM(atm_flux.shape, atm_flux.dtype),
             vmem((atm_blocks, tracer_count, cols)),
             vmem((3 * atm_blocks, tracer_count, cols)),
             vmem((levels, tracer_count, 2, cols)),
@@ -594,10 +619,11 @@
             vmem((64, cols)),
             vmem((64, cols)),
             vmem((2, tracer_count, rows, cols)),
+            vmem((2, 2, tracer_count, rows, cols)),
+            vmem((2, rows, cols)),
+            vmem((2, rows, cols)),
             vmem((2, tracer_count, rows, cols)),
-            vmem((rows, cols)),
-            vmem((rows, cols)),
-            vmem((tracer_count, rows, cols)),
+            vmem((2, tracer_count, rows, cols)),
             vmem((tracer_count, rows, cols)),
             vmem((levels, rows, cols)),
             vmem((levels, rows, cols)),
@@ -610,7 +636,7 @@
             vmem((3, 1, cols)),
             vmem((3, GROUP - 1, 1, cols)),
             vmem((2, 3 * rows, cols)),
-            pltpu.SemaphoreType.DMA((7,)),
+            pltpu.SemaphoreType.DMA((10,)),
             pltpu.SemaphoreType.DMA((COPIES,)),
             pltpu.SemaphoreType.DMA((COPIES,)),
         ],

time: 58.3 us -> 57.7 us (0.990)
  Pallas kernels: 53.6 us -> 53 us
    pallas_call x1, Pallas kernels: 53.6 us -> 53 us  [on_device(): pl.pallas_call(functools.partial(kernel, n_gy, n_gx), out_shape=(jax.Shap...]
where the time goes in v3:
time: 57.7 us; the launch traced here: 57.2 us
  Pallas kernels  53 us (92%)
  local copies, waits for them, and re-layouts  3.54 us (6%)
  between operations  0.64 us (1%)
    pallas_call x1, Pallas kernels, on_device(): pl.pallas_call(functools.partial(kernel, n_gy, n_gx), out_shape=(jax.Shap...  53 us
    unnamed x1, local copies, waits for them, and re-layouts  2.23 us
    slice x1, local copies, waits for them, and re-layouts, on_device(): return (new_tracers, in_slots[:1], in_slots[1:])  1.31 us

profile of v3, /device:TPU:1, one launch (start us, length us, event | category | flops | bytes accessed | tf_op | source)
XLA Modules:
  0.0 57.2 jit_solution(6638181715581245878)
XLA Ops:
  0.6 53.0 %ocean_window.1 = (f32[2,62,16,128]{3,2,1,0:T(8,128)}, f32[2,3,4,128]{3,2,1,0:T(4,128)}) custom-call(s32[1,2,16]{2,1,0:T(2,128)} %bitcast.2, s32[1,4]{1,0:T(1,128)} %bitcast.3, s32[1,96]{1,0:T(1,128)} %map_ref.1, bf16[1,2,2,128]{3,2,1,0:T(2,128)(2,1)} %atm_hbm.1, f32[16,128]{1,0:T(8,128)} %depth_hbm.1, f32[16,128]{1,0:T(8,128)} %surface_hbm.1, ...), custom_call_target="tpu_custom_call" | custom-call | tf_op jit(solution)/shard_map/ocean_window/pallas_call | solution.py:599
  53.6 1.3 %fusion = (f32[1,3,4,128]{3,2,1,0:T(4,128)}, f32[1,3,4,128]{3,2,1,0:T(4,128)}) fusion(f32[2,3,4,128]{3,2,1,0:T(4,128)} %get-tuple-element.6), kind=kLoop, calls=%fused_computation | loop fusion | bytes 24576 | tf_op jit(solution)/shard_map/slice | solution.py:659
  54.9 2.2 %copy.14 = f32[2,62,16,128]{3,2,1,0:T(8,128)} copy(f32[2,62,16,128]{3,2,1,0:T(8,128)} %get-tuple-element.12) | data formatting | bytes 2031616

commit v4 on v3

--- a/solution.py
+++ b/solution.py
@@ -417,7 +417,7 @@
             copy.wait_recv()
         lax.fori_loop(part * half, (part + 1) * half, put, 0, unroll=4)
         total = lax.fori_loop(
-            part * half, (part + 1) * half, functools.partial(advect, part), total, unroll=1
+            part * half, (part + 1) * half, functools.partial(advect, part), total, unroll=2
         )
     for f in range(tracer_count):
         solved[f, 0] = solved[f, 0] + surface_flux[f]

time: 57.7 us -> 51.3 us (0.89)
  Pallas kernels: 53 us -> 46.5 us
    pallas_call x1, Pallas kernels: 53 us -> 46.5 us  [on_device(): pl.pallas_call(functools.partial(kernel, n_gy, n_gx), out_shape=(jax.Shap...]
where the time goes in v4:
time: 51.3 us; the launch traced here: 50.7 us
  Pallas kernels  46.5 us (91%)
  local copies, waits for them, and re-layouts  3.54 us (7%)
  between operations  0.64 us (1%)
    pallas_call x1, Pallas kernels, on_device(): pl.pallas_call(functools.partial(kernel, n_gy, n_gx), out_shape=(jax.Shap...  46.5 us
    unnamed x1, local copies, waits for them, and re-layouts  2.23 us
    slice x1, local copies, waits for them, and re-layouts, on_device(): return (new_tracers, in_slots[:1], in_slots[1:])  1.31 us

profile of v4, /device:TPU:1, one launch (start us, length us, event | category | flops | bytes accessed | tf_op | source)
XLA Modules:
  0.0 50.7 jit_solution(1857244775846184331)
XLA Ops:
  0.6 46.5 %ocean_window.1 = (f32[2,62,16,128]{3,2,1,0:T(8,128)}, f32[2,3,4,128]{3,2,1,0:T(4,128)}) custom-call(s32[1,2,16]{2,1,0:T(2,128)} %bitcast.2, s32[1,4]{1,0:T(1,128)} %bitcast.3, s32[1,96]{1,0:T(1,128)} %map_ref.1, bf16[1,2,2,128]{3,2,1,0:T(2,128)(2,1)} %atm_hbm.1, f32[16,128]{1,0:T(8,128)} %depth_hbm.1, f32[16,128]{1,0:T(8,128)} %surface_hbm.1, ...), custom_call_target="tpu_custom_call" | custom-call | tf_op jit(solution)/shard_map/ocean_window/pallas_call | solution.py:599
  47.1 1.3 %fusion = (f32[1,3,4,128]{3,2,1,0:T(4,128)}, f32[1,3,4,128]{3,2,1,0:T(4,128)}) fusion(f32[2,3,4,128]{3,2,1,0:T(4,128)} %get-tuple-element.6), kind=kLoop, calls=%fused_computation | loop fusion | bytes 24576 | tf_op jit(solution)/shard_map/slice | solution.py:659
  48.5 2.2 %copy.14 = f32[2,62,16,128]{3,2,1,0:T(8,128)} copy(f32[2,62,16,128]{3,2,1,0:T(8,128)} %get-tuple-element.12) | data formatting | bytes 2031616

commit v5 on v4

--- a/solution.py
+++ b/solution.py
@@ -16,15 +16,6 @@
 SIDES = ((0, 1), (0, -1), (1, 0), (-1, 0), (1, 1), (1, -1), (-1, 1), (-1, -1))
 META, ATM, EDGE, SEARCH, SLOT, REDUCE = 0, 8, 10, 18, 26, 28
 COPIES = REDUCE + 3 * (GROUP - 1)
-
-
-def flux(speed, behind, centre, forward, beyond, mixing):
-    drop = centre - forward
-    return (
-        speed * (7.0 * (centre + forward) - (behind + beyond))
-        - jnp.abs(speed) * (3.0 * drop + (beyond - behind))
-        + mixing * drop
-    )
 
 
 def kernel(
@@ -62,7 +53,6 @@
     edge_near,
     speed_east,
     speed_west,
-    west_face,
     beyond,
     surface_flux,
     factor,
@@ -333,7 +323,7 @@
     east_open = centre(wide_east) * (1.0 / 12.0)
     north_open = centre(wide_north) * (1.0 / 12.0)
     south_open = centre(wide_south) * (1.0 / 12.0)
-    west_open = jnp.broadcast_to(centre(wide_west)[:, :1], (rows, cols)) * (1.0 / 12.0)
+    west_open = centre(wide_west) * (1.0 / 12.0)
     mask_south = wide_mask[6:8, cols : 2 * cols]
     mask_north = wide_mask[8 + rows : 10 + rows, cols : 2 * cols]
 
@@ -343,15 +333,6 @@
     for part in range(2):
         for f in range(tracer_count):
             behind = edge_near[1, part, f]
-            ahead = edge_own[part, f]
-            west_face[part, f] = flux(
-                speed_west[part] * west_open,
-                behind,
-                pltpu.roll(behind, cols - 1, 1),
-                pltpu.roll(ahead, cols - 2, 1),
-                pltpu.roll(ahead, cols - 3, 1),
-                (12.0 * DIFFUSIVITY) * west_open,
-            )
             beyond[part, f] = jnp.where(lane % 4 < 2, behind, edge_near[0, part, f])
 
     def coefficients(speed, mixing):
@@ -367,10 +348,15 @@
         back_s, centre_s, next_s, far_s = coefficients(
             north_speed[level, 7 : 7 + rows, :] * south_open, mix_south
         )
-        at_here = centre_n - next_s
+        turn = 4 * (level - part * half)
+        arriving = pltpu.roll(speed_west[part], cols - 1 - turn, 1)
+        speed = pltpu.roll(jnp.where(lane == cols - 1, arriving, east_speed[level]), 1, 1)
+        back_w, centre_w, next_w, far_w = coefficients(speed * west_open, mix_west)
+        at_here = (centre_n - next_s) + (centre_e - next_w)
+        at_east = next_e + far_w
+        at_west = back_e - centre_w
         at_north = next_n + far_s
         at_south = back_n - centre_s
-        turn = 4 * (level - part * half)
         results = []
         for f in range(tracer_count):
             here = cells[f, level, 8 : 8 + rows, :]
@@ -382,19 +368,16 @@
             east2 = pltpu.roll(jnp.where(lane < 2, outer, here), cols - 2, 1)
             east1 = pltpu.roll(jnp.where(lane < 1, outer, here), cols - 1, 1)
             west1 = pltpu.roll(jnp.where(lane == cols - 1, outer, here), 1, 1)
-            east_flux = (centre_e * here + next_e * east1) + (back_e * west1 - far_e * east2)
-            west_flux = jnp.where(
-                lane == 0,
-                pltpu.roll(west_face[part, f], lax.rem(cols - turn, cols), 1),
-                pltpu.roll(east_flux, 1, 1),
-            )
+            west2 = pltpu.roll(jnp.where(lane >= cols - 2, outer, here), 2, 1)
+            along = (at_east * east1 - far_e * east2) + (at_west * west1 - back_w * west2)
             spread = (at_here * here + at_north * north1) + (
                 at_south * south1 - (far_n * north2 + back_s * south2)
             )
-            results.append(mask * (here - (east_flux - west_flux) - spread))
+            results.append(mask * (here - along - spread))
         return results
 
     mix_east = (12.0 * DIFFUSIVITY) * east_open
+    mix_west = (12.0 * DIFFUSIVITY) * west_open
     mix_north = (12.0 * DIFFUSIVITY) * north_open
     mix_south = (12.0 * DIFFUSIVITY) * south_open
 
@@ -623,7 +606,6 @@
             vmem((2, rows, cols)),
             vmem((2, rows, cols)),
             vmem((2, tracer_count, rows, cols)),
-            vmem((2, tracer_count, rows, cols)),
             vmem((tracer_count, rows, cols)),
             vmem((levels, rows, cols)),
             vmem((levels, rows, cols)),

time: 51.3 us -> 49.3 us (0.961)
  Pallas kernels: 46.5 us -> 44.6 us
    pallas_call x1, Pallas kernels: 46.5 us -> 44.6 us  [on_device(): pl.pallas_call(functools.partial(kernel, n_gy, n_gx), out_shape=(jax.Shap...]
where the time goes in v5:
time: 49.3 us; the launch traced here: 48.8 us
  Pallas kernels  44.6 us (90%)
  local copies, waits for them, and re-layouts  3.54 us (7%)
  between operations  0.64 us (1%)
    pallas_call x1, Pallas kernels, on_device(): pl.pallas_call(functools.partial(kernel, n_gy, n_gx), out_shape=(jax.Shap...  44.6 us
    unnamed x1, local copies, waits for them, and re-layouts  2.23 us
    slice x1, local copies, waits for them, and re-layouts, on_device(): return (new_tracers, in_slots[:1], in_slots[1:])  1.31 us

profile of v5, /device:TPU:1, one launch (start us, length us, event | category | flops | bytes accessed | tf_op | source)
XLA Modules:
  0.0 48.8 jit_solution(17544677394329242243)
XLA Ops:
  0.6 44.6 %ocean_window.1 = (f32[2,62,16,128]{3,2,1,0:T(8,128)}, f32[2,3,4,128]{3,2,1,0:T(4,128)}) custom-call(s32[1,2,16]{2,1,0:T(2,128)} %bitcast.2, s32[1,4]{1,0:T(1,128)} %bitcast.3, s32[1,96]{1,0:T(1,128)} %map_ref.1, bf16[1,2,2,128]{3,2,1,0:T(2,128)(2,1)} %atm_hbm.1, f32[16,128]{1,0:T(8,128)} %depth_hbm.1, f32[16,128]{1,0:T(8,128)} %surface_hbm.1, ...), custom_call_target="tpu_custom_call" | custom-call | tf_op jit(solution)/shard_map/ocean_window/pallas_call | solution.py:582
  45.2 1.3 %fusion = (f32[1,3,4,128]{3,2,1,0:T(4,128)}, f32[1,3,4,128]{3,2,1,0:T(4,128)}) fusion(f32[2,3,4,128]{3,2,1,0:T(4,128)} %get-tuple-element.6), kind=kLoop, calls=%fused_computation | loop fusion | bytes 24576 | tf_op jit(solution)/shard_map/slice | solution.py:641
  46.5 2.2 %copy.14 = f32[2,62,16,128]{3,2,1,0:T(8,128)} copy(f32[2,62,16,128]{3,2,1,0:T(8,128)} %get-tuple-element.12) | data formatting | bytes 2031616
